TPU v7x, 32 devices: a whole 2x2x4 slice. The times are simulated.
32 devices in a mesh: lat: 8 (over y, x, core), lon: 4 (over z).
Axes of the slice: x: 2, y: 2, z: 4, core: 2. Of those that a mesh axis runs over, the one named last changes fastest.
Arguments:
- tracers: float32 [5, 16, 72, 1440], P(None, None, 'lat', 'lon'), may hold values from -6 to 6
- zonal_wind: float32 [16, 72, 1440], P(None, 'lat', 'lon'), may hold values from -0.45 to 0.45
- meridional_wind: float32 [16, 72, 1440], P(None, 'lat', 'lon'), may hold values from -0.45 to 0.45
- cutoff: int32 [72], P('lat'), may hold values from 1 to 720, as said below
Outputs:
- filtered: float32 [5, 16, 72, 1440], P(None, None, 'lat', 'lon')
Inputs may be any that keep to these rules, and one draw needn't show every extreme that they name: cutoff is 720 on every row at least 12 rows from both poles and below it on the rows nearer a pole; it is 1 on row 0 and row 71.
All inputs are finite; a program needn't handle non-finite values.
Results may differ from a plain program's by a relative error of at most 0.000075.
Values sent between devices are 32-bit elements; how exact they have to be, the bound alone decides.
No kernel may reach another device: no remote copies, remote signals or barrier semaphores. Data moves between devices by JAX's collectives and lax.ppermute only.
A program may use at most 64 MiB of HBM per device.

v0:
```python
import math

import jax
import jax.numpy as jnp
from jax import lax
from jax.sharding import PartitionSpec as P


def extended(block, sides, width):
    for axis, dim in sides:
        count = lax.axis_size(axis)
        forward = [(i, i + 1) for i in range(count - 1)]
        forward.append((count - 1, 0))
        backward = [(target, source) for source, target in forward]
        low = lax.ppermute(
            lax.slice_in_dim(block, block.shape[dim] - width, None, axis=dim), axis, forward
        )
        high = lax.ppermute(lax.slice_in_dim(block, 0, width, axis=dim), axis, backward)
        block = jnp.concatenate([low, block, high], axis=dim)
    return block


def from_behind(x, axis, by):
    count = lax.axis_size(axis)
    return lax.ppermute(x, axis, [(i, (i + by) % count) for i in range(count)])


def advect(q_pad, u_pad, v_pad):
    center = q_pad[..., 1:-1, 1:-1]
    u_mid = u_pad[..., 1:-1, 1:-1]
    east_speed = 0.5 * (u_mid + u_pad[..., 1:-1, 2:])
    west_speed = 0.5 * (u_pad[..., 1:-1, :-2] + u_mid)
    east_flux = (
        jnp.maximum(east_speed, 0.0) * center + jnp.minimum(east_speed, 0.0) * q_pad[..., 1:-1, 2:]
    )
    west_flux = (
        jnp.maximum(west_speed, 0.0) * q_pad[..., 1:-1, :-2] + jnp.minimum(west_speed, 0.0) * center
    )
    v_mid = v_pad[..., 1:-1, 1:-1]
    south_speed = 0.5 * (v_mid + v_pad[..., 2:, 1:-1])
    north_speed = 0.5 * (v_pad[..., :-2, 1:-1] + v_mid)
    south_flux = (
        jnp.maximum(south_speed, 0.0) * center
        + jnp.minimum(south_speed, 0.0) * q_pad[..., 2:, 1:-1]
    )
    north_flux = (
        jnp.maximum(north_speed, 0.0) * q_pad[..., :-2, 1:-1]
        + jnp.minimum(north_speed, 0.0) * center
    )
    return center - (east_flux - west_flux) - (south_flux - north_flux)


def table_rows(count, circle):
    lon_index = jnp.arange(count, dtype=jnp.int32)
    wave_number = jnp.arange(circle // 2 + 1, dtype=jnp.int32)
    phase = (lon_index[:, None] * wave_number[None, :] % circle).astype(jnp.float32) * (
        2.0 * math.pi / circle
    )
    return jnp.concatenate([jnp.cos(phase), jnp.sin(phase)], axis=1)


def spectral_scale(cut_rows, circle):
    half_lon = circle // 2
    wave_number = jnp.arange(half_lon + 1, dtype=jnp.int32)
    keep = (wave_number[None, :] <= cut_rows[:, None]).astype(jnp.float32)
    weight = jnp.where((wave_number == 0) | (wave_number == half_lon), 1.0, 2.0) / circle
    scaled = keep * weight[None, :]
    return jnp.concatenate([scaled, scaled], axis=1)


def inverse_rows(scaled, table):
    return lax.dot_general(
        scaled,
        table,
        (((1,), (1,)), ((), ())),
        precision=lax.Precision.HIGHEST,
        preferred_element_type=jnp.float32,
    )


def filter_circles(piece, cut_rows, circle):
    table = table_rows(circle, circle)
    coeffs = jnp.dot(
        piece, table, precision=lax.Precision.HIGHEST, preferred_element_type=jnp.float32
    )
    scaled = coeffs * spectral_scale(cut_rows, circle)
    return inverse_rows(scaled, table)


def body(tracers, zonal_wind, meridional_wind, cutoff):
    num_fields, num_levels, row_count, sector = tracers.shape
    field_planes = num_fields * num_levels
    planes = jnp.concatenate(
        [tracers.reshape(field_planes, row_count, sector), zonal_wind, meridional_wind], axis=0
    )
    padded = extended(planes, (("lat", 1), ("lon", 2)), 1)
    edges = jnp.stack([planes[:, 0, :], planes[:, -1, :]], axis=0)
    across = from_behind(edges, "lon", lax.axis_size("lon") // 2)
    flip = jnp.concatenate(
        [jnp.ones((field_planes + num_levels,), jnp.float32), -jnp.ones((num_levels,), jnp.float32)]
    )
    across = across * flip[None, :, None]
    lat_index = lax.axis_index("lat")
    top_row = jnp.where(lat_index == 0, across[0], padded[:, 0, 1:-1])
    bottom_row = jnp.where(lat_index == lax.axis_size("lat") - 1, across[1], padded[:, -1, 1:-1])
    padded = padded.at[:, 0, 1:-1].set(top_row).at[:, -1, 1:-1].set(bottom_row)
    q_pad = padded[:field_planes].reshape(num_fields, num_levels, row_count + 2, sector + 2)
    u_pad = padded[field_planes : field_planes + num_levels]
    v_pad = padded[field_planes + num_levels :]
    stepped = advect(q_pad, u_pad, v_pad)
    flat = stepped.reshape(field_planes * row_count, sector)
    n_sectors = lax.axis_size("lon")
    circle = sector * n_sectors
    polar = jnp.any(cutoff < circle // 2)
    cut_all = jnp.tile(cutoff, field_planes)
    lon_index = lax.axis_index("lon")
    share = lax.all_to_all(flat, "lon", split_axis=0, concat_axis=1, tiled=True)
    share_rows = share.shape[0]
    cut_rows = lax.dynamic_slice_in_dim(cut_all, lon_index * share_rows, share_rows, 0)
    done = lax.cond(polar, lambda: filter_circles(share, cut_rows, circle), lambda: share)
    result = lax.all_to_all(done, "lon", split_axis=1, concat_axis=0, tiled=True)
    return result.reshape(num_fields, num_levels, row_count, sector)


def solution(mesh):
    in_specs = (P(None, None, "lat", "lon"), P(None, "lat", "lon"), P(None, "lat", "lon"), P("lat"))
    out_specs = P(None, None, "lat", "lon")
    return jax.shard_map(body, mesh=mesh, in_specs=in_specs, out_specs=out_specs, check_vma=False)
```

profile of v0, /device:TPU:0, one launch (start us, length us, event | category | flops | bytes accessed | tf_op | source)
XLA Modules:
  0.0 137.9 jit_solution(16903622287517268346)
XLA Ops:
  0.0 1.4 copy.40
  1.4 0.5 collective-permute-start
  2.0 2.9 %collective-permute-start.1 = (f32[112,1,360]{2,0,1:T(8,128)S(1)}, f32[112,1,360]{2,0,1:T(8,128)S(1)}, u32[]{:S(2)}, u32[]{:S(2)}) collective-permute-start(f32[112,1,360]{2,0,1:T(8,128)S(1)} %get-tuple-element.77), channel_id=1, source_target_pairs={{4,0},{8,4},{12,8},{16,12},{20,16},{24,20},{28,24},{0,28},{5,1},{9... | collective-permute-start | bytes 483848 | tf_op jit(solution)/shard_map/ppermute | solution.py:18
  4.9 0.8 pad_maximum_fusion.13
  5.7 3.3 %collective-permute-start.4 = (f32[2,112,360]{2,1,0:T(8,128)}, f32[2,112,360]{2,1,0:T(8,128)}, u32[]{:S(2)}, u32[]{:S(2)}) collective-permute-start(f32[2,112,360]{2,1,0:T(8,128)} %pad_maximum_fusion.13), channel_id=1, source_target_pairs={{0,2},{1,3},{2,0},{3,1},{4,6},{5,7},{6,4},{7,5},{8,10},{9,11},{10,... | collective-permute-start | bytes 967688 | tf_op jit(solution)/shard_map/ppermute | solution.py:25
  9.0 0.7 copy-done.2
  9.9 0.4 copy-done.4
  10.8 3.4 %collective-permute-start.3 = (f32[112,11,1]{0,2,1:T(1,128)S(1)}, f32[112,11,1]{0,2,1:T(1,128)S(1)}, u32[]{:S(2)}, u32[]{:S(2)}) collective-permute-start(f32[112,11,1]{0,2,1:T(1,128)S(1)} %copy.42), channel_id=1, source_target_pairs={{1,0},{2,1},{3,2},{0,3},{5,4},{6,5},{7,6},{4,7},{9,8},{10,9},{11,1... | collective-permute-start | bytes 14792 | tf_op jit(solution)/shard_map/ppermute | solution.py:18
  14.1 0.6 fusion.29
  14.7 4.8 %collective-permute-done.2 = f32[112,11,1]{0,2,1:T(1,128)S(1)} collective-permute-done((f32[112,11,1]{0,2,1:T(1,128)S(1)}, f32[112,11,1]{0,2,1:T(1,128)S(1)}, u32[]{:S(2)}, u32[]{:S(2)}) %collective-permute-start.2) | collective-permute-done | bytes 4960 | tf_op jit(solution)/shard_map/ppermute | solution.py:15
  19.6 1.1 copy.43
  20.7 1.1 copy.44
  21.8 2.1 %pad_maximum_fusion.7 = f32[112,11,362]{2,0,1:T(8,128)S(1)} fusion(f32[112,11,1]{2,0,1:T(8,128)} %copy.44, f32[112,1,360]{2,0,1:T(8,128)} %copy-done.4, f32[16,9,360]{2,0,1:T(8,128)S(1)} %copy-done, f32[16,9,360]{2,0,1:T(8,128)S(1)} %copy-done.1, f32[80,9,360]{2,0,1:T(8,128)S(1)} %bitcast.25, f32[112,1,360]{2,0,1:T(8,128)} %copy-done.2, f32[112,11,1]{2,0,1:T(8,128)} %copy.43), kind=kLoop, calls=%fused_computation.38 | loop fusion | flops 2675904 | bytes 3567872 | tf_op jit(solution)/shard_map/concatenate | solution.py:19
  24.1 1.1 broadcast_multiply_fusion
  25.2 2.2 %scatter.6 = f32[112,11,362]{2,0,1:T(8,128)S(1)} dynamic-update-slice(f32[112,11,362]{2,0,1:T(8,128)S(1)} %pad_maximum_fusion.7, f32[112,1,360]{2,0,1:T(8,128)S(1)} %get-tuple-element.84, s32[]{:T(128)} %constant.117.clone.1, s32[]{:T(128)} %bitcast.5, s32[]{:T(128)} %bitcast.6) | dynamic-update-slice | bytes 322564 | tf_op jit(solution)/shard_map/scatter | solution.py:106
  27.5 1.0 scatter.9
  28.6 0.4 broadcast_maximum_fusion.3
  29.7 1.2 fusion.28
  30.9 2.7 %fusion.18 = f32[5,16,9,360]{3,2,1,0:T(8,128)S(1)} fusion(f32[5,16,9,360]{3,1,0,2:T(8,128)S(1)} %get-tuple-element.81, f32[5,16,9,360]{3,1,0,2:T(8,128)S(1)} %get-tuple-element.82, f32[5,16,9,360]{3,1,0,2:T(8,128)S(1)} %get-tuple-element.79, f32[5,16,9,360]{3,1,0,2:T(8,128)S(1)} %get-tuple-element.80, f32[5,16,9,360]{3,1,0,2:T(8,128)S(1)} %get-tuple-element.78, ...), kind=kLoop, calls=%fused_computation.30 | loop fusion | flops 4147200 | bytes 7879680 | tf_op jit(solution)/shard_map/sub | solution.py:50
  33.7 1.2 all_to_all.29
  34.9 8.3 %all-to-all-start = ((f32[4,180,360]{2,1,0:T(8,128)}), f32[4,180,360]{2,1,0:T(8,128)S(1)}, u32[]{:S(2)}, u32[]{:S(2)}) async-start(f32[4,180,360]{2,1,0:T(8,128)} %all_to_all.29), calls=%async_computation | async-start | bytes 2260992 | tf_op jit(solution)/shard_map/all_to_all | solution.py:117
  43.2 0.6 compare_reduce_fusion
  44.5 26.1 %all-to-all-done = f32[4,180,360]{2,1,0:T(8,128)S(1)} async-done(((f32[4,180,360]{2,1,0:T(8,128)}), f32[4,180,360]{2,1,0:T(8,128)S(1)}, u32[]{:S(2)}, u32[]{:S(2)}) %all-to-all-start) | async-done | bytes 1036832 | tf_op jit(solution)/shard_map/all_to_all | solution.py:117
  70.6 0.3 copy.58
  70.9 0.6 all_to_all.32
  71.5 34.6 %conditional.1 = (f32[180,1440]{1,0:T(8,128)S(1)}) conditional(s32[]{:T(128)} %convert_element_type.10, f32[180,1440]{1,0:T(8,128)S(1)} %all_to_all.32, (f32[180,1440]{1,0:T(8,128)S(1)}, s32[9]{0:T(128)S(1)}, s32[]{:T(128)}) %tuple.42), branch_computations={%region_1.2_spmd, %region_2.3_spmd} | conditional | flops 8984673280 | bytes 30122742 | solution.py:120
  72.0 18.4 %fusion.6 = (f32[1440,721]{1,0:T(8,128)S(1)}, f32[1440,721]{1,0:T(8,128)S(1)}) fusion(), kind=kLoop, calls=%fused_computation.9 | loop fusion | flops 9344160 | bytes 8305920 | tf_op jit(solution)/shard_map/cond/branch_1_fun/sin | solution.py:59
  90.5 6.8 %fusion.10 = f32[180,1442]{1,0:T(8,128)S(1)} fusion(f32[180,1440]{1,0:T(8,128)S(1)} %get-tuple-element.61, f32[1440,721]{1,0:T(8,128)S(1)} %get-tuple-element.64, f32[1440,721]{1,0:T(8,128)S(1)} %get-tuple-element.65, f32[180,721]{1,0:T(8,128)S(1)} %fusion.11), kind=kOutput, calls=%fused_computation.13 | convolution fusion | flops 4487792640 | bytes 10900080 | tf_op jit(solution)/shard_map/cond/branch_1_fun/dot_general | solution.py:83
  97.3 8.5 %fusion = f32[180,1440]{1,0:T(8,128)S(1)} fusion(f32[180,1442]{1,0:T(8,128)S(1)} %fusion.10, f32[1440,721]{1,0:T(8,128)S(1)} %get-tuple-element.64, f32[1440,721]{1,0:T(8,128)S(1)} %get-tuple-element.65), kind=kOutput, calls=%fused_computation.1 | convolution fusion | flops 4487273472 | bytes 10380960 | tf_op jit(solution)/shard_map/cond/branch_1_fun/dot_general | solution.py:72
  106.1 0.8 all_to_all.33
  107.0 29.4 %all_to_all.38 = f32[180,4,360]{2,0,1:T(8,128)S(1)} all-to-all(f32[180,4,360]{2,0,1:T(8,128)S(1)} %copy.59), channel_id=1, replica_groups=mesh['lat'=8,'lon'=4] {'lon'}, dimensions={1} | all-to-all | bytes 2073600 | tf_op jit(solution)/shard_map/all_to_all | solution.py:121
  136.6 1.3 copy.60
  (41 shorter events, 2.3 us)
Async XLA Ops:
  0.0 1.4 copy-start
  0.0 1.4 %copy-start.1 = (f32[16,9,360]{2,0,1:T(8,128)S(1)}, f32[16,9,360]{2,0,1:T(8,128)}, u32[]{:S(2)}) copy-start(f32[16,9,360]{2,0,1:T(8,128)} %param.11) | copy-start | bytes 622084
  1.4 7.5 %collective-permute-start = (f32[112,1,360]{2,0,1:T(8,128)S(1)}, f32[112,1,360]{2,0,1:T(8,128)S(1)}, u32[]{:S(2)}, u32[]{:S(2)}) collective-permute-start(f32[112,1,360]{2,0,1:T(8,128)S(1)} %get-tuple-element.76), channel_id=1, source_target_pairs={{0,4},{4,8},{8,12},{12,16},{16,20},{20,24},{24,28},{28,0},{1,5},{5... | collective-permute-start | bytes 483848 | tf_op jit(solution)/shard_map/ppermute | solution.py:15
  2.0 7.0 %collective-permute-start.1 = (f32[112,1,360]{2,0,1:T(8,128)S(1)}, f32[112,1,360]{2,0,1:T(8,128)S(1)}, u32[]{:S(2)}, u32[]{:S(2)}) collective-permute-start(f32[112,1,360]{2,0,1:T(8,128)S(1)} %get-tuple-element.77), channel_id=1, source_target_pairs={{4,0},{8,4},{12,8},{16,12},{20,16},{24,20},{28,24},{0,28},{5,1},{9... | collective-permute-start | bytes 483848 | tf_op jit(solution)/shard_map/ppermute | solution.py:18
  5.7 18.4 %collective-permute-start.4 = (f32[2,112,360]{2,1,0:T(8,128)}, f32[2,112,360]{2,1,0:T(8,128)}, u32[]{:S(2)}, u32[]{:S(2)}) collective-permute-start(f32[2,112,360]{2,1,0:T(8,128)} %pad_maximum_fusion.13), channel_id=1, source_target_pairs={{0,2},{1,3},{2,0},{3,1},{4,6},{5,7},{6,4},{7,5},{8,10},{9,11},{10,... | collective-permute-start | bytes 967688 | tf_op jit(solution)/shard_map/ppermute | solution.py:25
  9.0 0.7 copy-start.2
  9.7 0.7 copy-start.4
  10.8 9.9 %collective-permute-start.3 = (f32[112,11,1]{0,2,1:T(1,128)S(1)}, f32[112,11,1]{0,2,1:T(1,128)S(1)}, u32[]{:S(2)}, u32[]{:S(2)}) collective-permute-start(f32[112,11,1]{0,2,1:T(1,128)S(1)} %copy.42), channel_id=1, source_target_pairs={{1,0},{2,1},{3,2},{0,3},{5,4},{6,5},{7,6},{4,7},{9,8},{10,9},{11,1... | collective-permute-start | bytes 14792 | tf_op jit(solution)/shard_map/ppermute | solution.py:18
  14.1 5.4 %collective-permute-start.2 = (f32[112,11,1]{0,2,1:T(1,128)S(1)}, f32[112,11,1]{0,2,1:T(1,128)S(1)}, u32[]{:S(2)}, u32[]{:S(2)}) collective-permute-start(f32[112,11,1]{0,2,1:T(1,128)S(1)} %copy.41), channel_id=1, source_target_pairs={{0,1},{1,2},{2,3},{3,0},{4,5},{5,6},{6,7},{7,4},{8,9},{9,10},{10,1... | collective-permute-start | bytes 14792 | tf_op jit(solution)/shard_map/ppermute | solution.py:15
  21.8 2.3 %copy-start.6 = (f32[112]{0:T(128)S(1)}, f32[112]{0:T(128)}, u32[]{:S(2)}) copy-start(f32[112]{0:T(128)} %constant.118.clone.1) | copy-start | bytes 1348
  21.8 3.4 %copy-start.3 = (f32[112,1,360]{2,0,1:T(8,128)S(1)}, f32[112,1,360]{2,0,1:T(8,128)}, u32[]{:S(2)}) copy-start(f32[112,1,360]{2,0,1:T(8,128)} %copy-done.2) | copy-start | bytes 483844
  21.8 3.4 %copy-start.5 = (f32[112,1,360]{2,0,1:T(8,128)S(1)}, f32[112,1,360]{2,0,1:T(8,128)}, u32[]{:S(2)}) copy-start(f32[112,1,360]{2,0,1:T(8,128)} %copy-done.4) | copy-start | bytes 483844
  34.9 8.3 %copy-start.7 = (s32[9]{0:T(128)S(1)}, s32[9]{0:T(128)}, u32[]{:S(2)}) copy-start(s32[9]{0:T(128)} %param.13) | copy-start | bytes 112
  34.9 35.7 %all-to-all-start = ((f32[4,180,360]{2,1,0:T(8,128)}), f32[4,180,360]{2,1,0:T(8,128)S(1)}, u32[]{:S(2)}, u32[]{:S(2)}) async-start(f32[4,180,360]{2,1,0:T(8,128)} %all_to_all.29), calls=%async_computation | async-start | bytes 2260992 | tf_op jit(solution)/shard_map/all_to_all | solution.py:117
where the time goes:
time: 138 us
  waiting for transfers between devices  31.1 us (23%)
  blocking collectives  29.4 us (21%)
  other arithmetic  26.6 us (19%)
  starting transfers between devices  18.4 us (13%)
  local copies, waits for them, and re-layouts  15.7 us (11%)
  matrix products  15.3 us (11%)
    all_to_all x1, blocking collectives, body(): lax.all_to_all(done, 'lon', split_axis=1, concat_axis=0, tiled=True)  29.4 us
    all_to_all x1, waiting for transfers between devices, body(): share = lax.all_to_all(flat, 'lon', split_axis=0, concat_axis=1, tiled=True)  26.1 us
    sin x1, other arithmetic, table_rows(): return jnp.concatenate([jnp.cos(phase), jnp.sin(phase)], axis=1)  18.4 us
    dot_general x1, matrix products, inverse_rows(): lax.dot_general(scaled, table, (((1,), (1,)), ((), ())), precision=lax.Pr...  8.49 us
    all_to_all x1, starting transfers between devices, body(): share = lax.all_to_all(flat, 'lon', split_axis=0, concat_axis=1, tiled=True)  8.33 us
    dot_general x1, matrix products, filter_circles(): jnp.dot(piece, table, precision=lax.Precision.HIGHEST, preferred_element_...  6.82 us
    ppermute x2, starting transfers between devices, extended(): lax.ppermute(lax.slice_in_dim(block, 0, width, axis=dim), axis, backward)  6.29 us
    ppermute x2, waiting for transfers between devices, extended(): lax.ppermute(lax.slice_in_dim(block, block.shape[dim] - width, None, axis...  4.83 us
  transfers between devices with their start and end apart: 6, of which 3 were waited for; matrix products, arithmetic and copies ran while one was open for 5% of the time, Pallas kernels for 0%

commit v1 on v0

v1 whole, which is shorter than its diff:
```python
import math

import jax
import jax.numpy as jnp
from jax import lax
from jax.experimental import pallas as pl
from jax.experimental.pallas import tpu as pltpu
from jax.sharding import PartitionSpec as P

LANES = 128
EDGES = 4


class Plan:
    def __init__(self, fields, levels, rows, sector, n_lat, n_lon):
        self.fields, self.levels, self.rows, self.sector = fields, levels, rows, sector
        self.n_lat, self.n_lon = n_lat, n_lon
        self.planes = fields * levels
        self.circle = sector * n_lon
        self.quarter = self.circle // 4
        cap = rows * n_lat // 6
        self.full = (cap - 1) // rows
        self.n_x = cap - self.full * rows
        self.n_y = rows - self.n_x
        self.width = -(-(sector + EDGES) // LANES) * LANES
        self.x_count = self.n_x * self.planes // n_lon
        self.y_count = self.n_y * self.planes // n_lon
        self.x_full = [0] + list(range(1 + self.n_y, rows))

    def pieces(self, index, count):
        start, out = index * self.planes, []
        stop = start + self.planes
        while start < stop:
            chunk, offset = divmod(start, count)
            size = min(count - offset, stop - start)
            out.append((chunk, offset, start - index * self.planes, size))
            start += size
        return out

    def x_row(self, index, lat):
        full = (lat < self.full) | (lat >= self.n_lat - self.full)
        south = lat >= self.n_lat // 2
        partial = jnp.where(south, self.rows - self.n_x + index, index)
        return jnp.where(full, self.x_full[index], partial)


def split_speed(speed):
    return jnp.maximum(speed, 0.0), jnp.minimum(speed, 0.0)


def tiled(x, fields):
    return jnp.concatenate([x] * fields, axis=0) if fields > 1 else x


def back(x, width):
    return pltpu.roll(x, width - 1, 1)


def inner_rows_kernel(plan, q_ref, u_ref, v_ref, *refs):
    outs, buf, q_pad, u_pad = refs[: plan.n_lon], *refs[plan.n_lon :]
    width, sector = plan.width, plan.sector
    lane = lax.broadcasted_iota(jnp.int32, (plan.levels, width), 1)
    inside = lane < sector - 1
    q_pad[...] = jnp.zeros_like(q_pad)
    u_pad[...] = jnp.zeros_like(u_pad)
    wide = lax.broadcasted_iota(jnp.int32, (plan.planes, width), 1)

    def south_flux(r):
        plus, minus = split_speed(0.5 * (v_ref[r] + v_ref[r + 1]))
        return tiled(plus, plan.fields) * q_ref[r] + tiled(minus, plan.fields) * q_ref[r + 1]

    north = south_flux(0)
    for i in range(plan.n_y):
        r = 1 + i
        q_pad[:, 0:sector] = q_ref[r]
        u_pad[:, 0:sector] = u_ref[r]
        q, u = q_pad[...], u_pad[...]
        plus, minus = split_speed(0.5 * (u + back(u, width)))
        plus, minus = jnp.where(inside, plus, 0.0), jnp.where(inside, minus, 0.0)
        east = tiled(plus, plan.fields) * q + tiled(minus, plan.fields) * back(q, width)
        stepped = q - (east - pltpu.roll(east, 1, 1))
        south = south_flux(r)
        first_u, last_u = tiled(u[:, 0:1], plan.fields), tiled(u[:, sector - 1 : sector], plan.fields)
        stepped = jnp.where(wide == sector, q[:, 0:1], stepped)
        stepped = jnp.where(wide == sector + 1, q[:, sector - 1 : sector], stepped)
        stepped = jnp.where(wide == sector + 2, first_u, stepped)
        stepped = jnp.where(wide == sector + 3, last_u, stepped)
        q_pad[...] = stepped
        q_pad[:, 0:sector] = q_pad[:, 0:sector] - (south - north)
        for chunk, offset, first, size in plan.pieces(i, plan.y_count):
            buf[chunk, offset : offset + size, :] = q_pad[first : first + size, :]
        north = south
    lon = lax.axis_index("lon")
    for s in range(plan.n_lon):
        outs[s][...] = buf[lax.rem(lon + s, plan.n_lon)]


def all_rows_kernel(plan, q_ref, u_ref, v_ref, one_ref, two_ref, west_ref, east_ref, *refs):
    outs, done, buf, q_pad, u_pad, stage = refs[: plan.n_lon], *refs[plan.n_lon :]
    width, sector, planes, rows = plan.width, plan.sector, plan.planes, plan.rows
    lat = lax.axis_index("lat")
    odd = lax.rem(lat, 2) == 1
    sign_north = jnp.where(lat == 0, -1.0, 1.0)
    sign_south = jnp.where(lat == plan.n_lat - 1, -1.0, 1.0)
    one, two = one_ref[...], two_ref[...]
    above, below = jnp.where(odd, two, one), jnp.where(odd, one, two)
    q_above, v_above = above[:planes], above[planes:] * sign_north
    q_below, v_below = below[:planes], below[planes:] * sign_south
    q_pad[...] = jnp.zeros_like(q_pad)
    u_pad[...] = jnp.zeros_like(u_pad)

    def face(v_low, v_high, q_low, q_high):
        plus, minus = split_speed(0.5 * (v_low + v_high))
        return tiled(plus, plan.fields) * q_low + tiled(minus, plan.fields) * q_high

    north = face(v_above, v_ref[0], q_above, q_ref[0])
    for r in range(rows):
        q_pad[:, 0:sector] = q_ref[r]
        u_pad[:, 0:sector] = u_ref[r]
        q_pad[:, sector : sector + 1] = east_ref[:planes, r : r + 1]
        u_pad[:, sector : sector + 1] = east_ref[planes:, r : r + 1]
        q_pad[:, width - 1 : width] = west_ref[:planes, r : r + 1]
        u_pad[:, width - 1 : width] = west_ref[planes:, r : r + 1]
        q, u = q_pad[...], u_pad[...]
        plus, minus = split_speed(0.5 * (u + back(u, width)))
        east = tiled(plus, plan.fields) * q + tiled(minus, plan.fields) * back(q, width)
        stage[r] = q - (east - pltpu.roll(east, 1, 1))
        if r + 1 < rows:
            south = face(v_ref[r], v_ref[r + 1], q_ref[r], q_ref[r + 1])
        else:
            south = face(v_ref[r], v_below, q_ref[r], q_below)
        value = stage[r, :, 0:sector] - (south - north)
        stage[r, :, 0:sector] = value
        done[r] = value
        north = south
    for j in range(plan.n_x):
        r = plan.x_row(j, lat)
        for chunk, offset, first, size in plan.pieces(j, plan.x_count):
            buf[chunk, offset : offset + size, :] = stage[r, first : first + size, :]
    lon = lax.axis_index("lon")
    for s in range(plan.n_lon):
        outs[s][...] = buf[lax.rem(lon + s, plan.n_lon)]


def product(x, table_hi, table_lo, transposed):
    dims = (((1,), (1 if transposed else 0,)), ((), ()))
    x_hi = x.astype(jnp.bfloat16)
    x_lo = (x - x_hi.astype(jnp.float32)).astype(jnp.bfloat16)
    count = x.shape[0]
    both = lax.dot_general(
        jnp.concatenate([x_hi, x_lo], axis=0), table_hi, dims, preferred_element_type=jnp.float32
    )
    low = lax.dot_general(x_hi, table_lo, dims, preferred_element_type=jnp.float32)
    return both[:count] + both[count:] + low


def filter_quarters(plan, quarters, cut, hi, lo):
    x0, x1, x2, x3 = quarters
    a, b, u, v = x0 + x2, x1 + x3, x0 - x2, x1 - x3
    count, size, circle = x0.shape[0], plan.quarter, plan.circle
    m = lax.broadcasted_iota(jnp.int32, (count, size), 1)

    def kept(h, r):
        k = 4 * m + r
        return jnp.where(jnp.minimum(k, circle - k) <= cut, h, 0.0) * (1.0 / circle)

    def times(x, i, transposed=False):
        return product(x, hi[i], lo[i], transposed)

    h0 = kept(times(a + b, 0), 0)
    h2 = kept(times(a - b, 1), 2)
    h1 = kept(times(u, 2) + times(v, 4), 1)
    h3 = kept(times(u, 3) + times(v, 5), 3)
    even, twice = times(h0, 0, True), times(h2, 1, True)
    o_u = times(h1, 2, True) + times(h3, 3, True)
    o_v = times(h1, 4, True) + times(h3, 5, True)
    both, apart = even + twice, even - twice
    return both + o_u, apart + o_v, both - o_u, apart - o_v


def filter_kernel(plan, count, row_of, with_edges, cut_ref, hi_ref, lo_ref, *refs):
    n = plan.n_lon
    ins, outs = refs[:n], refs[n : 2 * n]
    sector = plan.sector
    lat, lon = lax.axis_index("lat"), lax.axis_index("lon")
    circle_index = lon * count + lax.broadcasted_iota(jnp.int32, (count, 1), 0)
    cut = jnp.full((count, 1), plan.circle, jnp.int32)
    rows_here = (plan.n_y if with_edges else plan.n_x)
    for i in range(rows_here):
        here = (circle_index >= i * plan.planes) & (circle_index < (i + 1) * plan.planes)
        cut = jnp.where(here, cut_ref[row_of(i, lat)], cut)
    pieces = [ref[:, 0:sector] for ref in ins]
    if with_edges:
        tails = [ref[:, sector : sector + EDGES] for ref in ins]
        lane = lax.broadcasted_iota(jnp.int32, (count, sector), 1)
        fluxes = []
        for j in range(n):
            here, there = tails[j], tails[(j + 1) % n]
            plus, minus = split_speed(0.5 * (here[:, 3:4] + there[:, 2:3]))
            fluxes.append(plus * here[:, 1:2] + minus * there[:, 0:1])
        pieces = [
            piece - jnp.where(lane == sector - 1, fluxes[j], 0.0) + jnp.where(lane == 0, fluxes[j - 1], 0.0)
            for j, piece in enumerate(pieces)
        ]
    per = n // 4
    quarters = [
        jnp.concatenate(pieces[per * i : per * (i + 1)], axis=1) if per > 1 else pieces[i] for i in range(4)
    ]
    filtered = filter_quarters(plan, quarters, cut, hi_ref, lo_ref)
    for j in range(n):
        part = j % per
        outs[j][...] = filtered[j // per][:, part * sector : (part + 1) * sector]


def merge_kernel(plan, stepped_ref, *refs):
    n = plan.n_lon
    y_ins, x_ins, out, buf = refs[:n], refs[n : 2 * n], refs[2 * n], refs[2 * n + 1]
    lat, lon = lax.axis_index("lat"), lax.axis_index("lon")
    full = (lat < plan.full) | (lat >= plan.n_lat - plan.full)
    part = (lat == plan.full) | (lat == plan.n_lat - 1 - plan.full)

    @pl.when(jnp.logical_not(full))
    def _():
        out[...] = stepped_ref[...]

    @pl.when(full)
    def _():
        for j in range(n):
            buf[lax.rem(lon + n - j, n), 0 : plan.y_count, :] = y_ins[j][...]
        for i in range(plan.n_y):
            for chunk, offset, first, size in plan.pieces(i, plan.y_count):
                out[1 + i, first : first + size, :] = buf[chunk, offset : offset + size, :]

    @pl.when(full | part)
    def _():
        for j in range(n):
            buf[lax.rem(lon + n - j, n), 0 : plan.x_count, :] = x_ins[j][...]
        for i in range(plan.n_x):
            r = plan.x_row(i, lat)
            for chunk, offset, first, size in plan.pieces(i, plan.x_count):
                out[r, first : first + size, :] = buf[chunk, offset : offset + size, :]


def call(kernel, outs, scratch=(), **options):
    return pl.pallas_call(
        kernel,
        out_shape=[jax.ShapeDtypeStruct(shape, jnp.float32) for shape in outs],
        **options,
        scratch_shapes=[pltpu.VMEM(shape, jnp.float32) for shape in scratch],
    )


def transform_tables(plan):
    size, circle = plan.quarter, plan.circle
    inner = max(d for d in range(8, 41, 8) if size % d == 0)
    outer = size // inner
    m = 4 * jnp.arange(size, dtype=jnp.int32)
    k = jnp.stack([m, m + 2, m + 1, m + 3, -(m + 1), -(m + 3)])
    sign = jnp.array([1.0, 1.0, 1.0, 1.0, 1.0, -1.0], jnp.float32)[:, None, None, None]

    def angle(count, step):
        n = step * jnp.arange(count, dtype=jnp.int32)
        return jnp.mod(k[:, None, :] * n[None, :, None], circle).astype(jnp.float32) * (2.0 * math.pi / circle)

    coarse, fine = angle(outer, inner), angle(inner, 1)
    cos_c, sin_c = jnp.cos(coarse)[:, :, None, :], jnp.sin(coarse)[:, :, None, :]
    cos_f, sin_f = jnp.cos(fine)[:, None, :, :], jnp.sin(fine)[:, None, :, :]
    table = sign * (cos_c * (cos_f + sin_f) + sin_c * (cos_f - sin_f))
    table = table.reshape(6, size, size)
    high = lax.reduce_precision(table, 8, 7)
    return high.astype(jnp.bfloat16), (table - high).astype(jnp.bfloat16)


def body(tracers, zonal_wind, meridional_wind, cutoff):
    fields, levels, rows, sector = tracers.shape
    n_lat, n_lon = lax.axis_size("lat"), lax.axis_size("lon")
    plan = Plan(fields, levels, rows, sector, n_lat, n_lon)
    planes, width = plan.planes, plan.width
    q = tracers.reshape(planes, rows, sector)
    u, v = zonal_wind, meridional_wind
    lat_index = lax.axis_index("lat")
    both = ("lat", "lon")

    def device(lat, lon):
        return lat * n_lon + lon % n_lon

    def shift_pairs(lats, by):
        return [(device(a, z), device(a, z + by)) for a in lats for z in range(n_lon)]

    full_lats = list(range(plan.full)) + list(range(n_lat - plan.full, n_lat))
    polar_lats = list(range(plan.full + 1)) + list(range(n_lat - plan.full - 1, n_lat))

    qt, ut, vt = (jnp.transpose(x, (1, 0, 2)) for x in (q, u, v))

    odd = lax.rem(lat_index, 2)
    qv = jnp.concatenate([qt[0], vt[0]], axis=0), jnp.concatenate([qt[-1], vt[-1]], axis=0)
    toward_one = jnp.where(odd == 1, qv[1], qv[0])
    toward_two = jnp.where(odd == 1, qv[0], qv[1])
    pairs_one = shift_pairs((0, n_lat - 1), n_lon // 2)
    for a in range(1, n_lat - 1, 2):
        for z in range(n_lon):
            pairs_one += [(device(a, z), device(a + 1, z)), (device(a + 1, z), device(a, z))]
    pairs_two = [(device(a, z), device(a ^ 1, z)) for a in range(n_lat) for z in range(n_lon)]
    two = lax.ppermute(toward_two, both, pairs_two)
    one = lax.ppermute(toward_one, both, pairs_one)

    y_send = call(
        lambda *refs: inner_rows_kernel(plan, *refs),
        [(plan.y_count, width)] * n_lon,
        [(n_lon, plan.y_count, width), (planes, width), (levels, width)],
    )(qt, ut, vt)
    y_got = [y_send[0]] + [
        lax.ppermute(y_send[s], both, shift_pairs(full_lats, s)) for s in range(1, n_lon)
    ]

    last = jnp.concatenate([q[:, :, -1], u[:, :, -1]], axis=0)
    first = jnp.concatenate([q[:, :, 0], u[:, :, 0]], axis=0)
    west = lax.ppermute(last, "lon", [(i, (i + 1) % n_lon) for i in range(n_lon)])
    east = lax.ppermute(first, "lon", [(i, (i - 1) % n_lon) for i in range(n_lon)])

    *x_send, stepped = call(
        lambda *refs: all_rows_kernel(plan, *refs),
        [(plan.x_count, width)] * n_lon + [(rows, planes, sector)],
        [(n_lon, plan.x_count, width), (planes, width), (levels, width), (rows, planes, width)],
    )(qt, ut, vt, one, two, west, east)
    x_got = [x_send[0]] + [
        lax.ppermute(x_send[s], both, shift_pairs(polar_lats, s)) for s in range(1, n_lon)
    ]

    hi, lo = transform_tables(plan)
    vmem = pl.BlockSpec(memory_space=pltpu.VMEM)
    smem = pl.BlockSpec(memory_space=pltpu.SMEM)

    def filtered(got, count, row_of, with_edges, lats):
        ordered = [got[(n_lon - j) % n_lon] for j in range(n_lon)]
        pieces = call(
            lambda *refs: filter_kernel(plan, count, row_of, with_edges, *refs),
            [(count, sector)] * n_lon,
            in_specs=[smem] + [vmem] * (2 + n_lon),
        )(cutoff, hi, lo, *ordered)
        return [pieces[0]] + [
            lax.ppermute(pieces[s], both, shift_pairs(lats, s)) for s in range(1, n_lon)
        ]

    y_back = filtered(y_got, plan.y_count, lambda i, lat: 1 + i, True, full_lats)
    x_back = filtered(x_got, plan.x_count, plan.x_row, False, polar_lats)
    (merged,) = call(
        lambda *refs: merge_kernel(plan, *refs),
        [(rows, planes, sector)],
        [(n_lon, max(plan.y_count, plan.x_count), sector)],
    )(stepped, *y_back, *x_back)
    return jnp.transpose(merged, (1, 0, 2)).reshape(fields, levels, rows, sector)


def solution(mesh):
    in_specs = (P(None, None, "lat", "lon"), P(None, "lat", "lon"), P(None, "lat", "lon"), P("lat"))
    out_specs = P(None, None, "lat", "lon")
    return jax.shard_map(body, mesh=mesh, in_specs=in_specs, out_specs=out_specs, check_vma=False)
```

time: 138 us -> 88.5 us (0.64)
  starting transfers between devices: 18.4 us -> 48.1 us
  blocking collectives: 29.4 us -> 0 us
  waiting for transfers between devices: 31.1 us -> 3.93 us
  Pallas kernels: 0 us -> 21.5 us
  other arithmetic: 26.6 us -> 6.02 us
  matrix products: 15.3 us -> 0 us
  local copies, waits for them, and re-layouts: 15.7 us -> 7.88 us
    ppermute x5 -> x16, starting transfers between devices: 10.1 us -> 48.1 us  [the longest x6 21.1 us: filtered(): lax.ppermute(pieces[s], both, shift_pairs(lats, s))]
    all_to_all x1 -> x0, blocking collectives: 29.4 us -> none  [body(): lax.all_to_all(done, 'lon', split_axis=1, concat_axis=0, tiled=True)]
    all_to_all x1 -> x0, waiting for transfers between devices: 26.1 us -> none  [body(): share = lax.all_to_all(flat, 'lon', split_axis=0, concat_axis=1, tiled=True)]
    pallas_call x0 -> x5, Pallas kernels: none -> 21.5 us  [the longest x2 10.5 us: filtered(): call(lambda *refs: filter_kernel(plan, count, row_of, with_edges, *refs),...]
    sin x1 -> x0, other arithmetic: 18.4 us -> none  [table_rows(): return jnp.concatenate([jnp.cos(phase), jnp.sin(phase)], axis=1)]
    dot_general x2 -> x0, matrix products: 15.3 us -> none  [the longest x1 8.49 us: inverse_rows(): lax.dot_general(scaled, table, (((1,), (1,)), ((), ())), precision=lax.Pr...]
    all_to_all x1 -> x0, starting transfers between devices: 8.33 us -> none  [body(): share = lax.all_to_all(flat, 'lon', split_axis=0, concat_axis=1, tiled=True)]
    scatter x2 -> x0, local copies, waits for them, and re-layouts: 3.25 us -> none  [body(): padded = padded.at[:, 0, 1:-1].set(top_row).at[:, -1, 1:-1].set(bottom_row)]
  transfers between devices with their start and end apart: 6 -> 16, of which waited for: 3 -> 2; matrix products, arithmetic and copies ran while one was open for 5% -> 9% of each run, Pallas kernels for 0% -> 16%
where the time goes in v1:
time: 88.5 us; the launch traced here: 87.7 us
  starting transfers between devices  48.1 us (54%)
  Pallas kernels  21.5 us (24%)
  local copies, waits for them, and re-layouts  7.88 us (9%)
  other arithmetic  6.02 us (7%)
  waiting for transfers between devices  3.93 us (4%)
    ppermute x6, starting transfers between devices, filtered(): lax.ppermute(pieces[s], both, shift_pairs(lats, s))  21.1 us
    ppermute x3, starting transfers between devices, body(): lax.ppermute(y_send[s], both, shift_pairs(full_lats, s))  10.6 us
    pallas_call x2, Pallas kernels, filtered(): call(lambda *refs: filter_kernel(plan, count, row_of, with_edges, *refs),...  10.5 us
    ppermute x3, starting transfers between devices, body(): lax.ppermute(x_send[s], both, shift_pairs(polar_lats, s))  10.3 us
    ppermute x1, starting transfers between devices, body(): lax.ppermute(first, 'lon', [(i, (i - 1) % n_lon) for i in range(n_lon)])  5.13 us
    pallas_call x1, Pallas kernels, body(): call(lambda *refs: all_rows_kernel(plan, *refs), [(plan.x_count, width)]...  4.65 us
    ppermute x6, waiting for transfers between devices, filtered(): lax.ppermute(pieces[s], both, shift_pairs(lats, s))  3.9 us
    pallas_call x1, Pallas kernels, body(): call(lambda *refs: inner_rows_kernel(plan, *refs), [(plan.y_count, width)...  3.54 us
  transfers between devices with their start and end apart: 16, of which 2 were waited for; matrix products, arithmetic and copies ran while one was open for 9% of the time, Pallas kernels for 16%

profile of v1, /device:TPU:0, one launch (start us, length us, event | category | flops | bytes accessed | tf_op | source)
XLA Modules:
  0.0 87.7 jit_solution(588966208054698843)
XLA Ops:
  0.0 1.0 %fusion.21 = (f32[16,9,1]{2,0,1:T(8,128)S(1)}, f32[16,9,1]{2,0,1:T(8,128)S(1)}) fusion(f32[16,9,360]{2,0,1:T(8,128)} %param.6), kind=kLoop, calls=%fused_computation.44 | loop fusion | bytes 2304 | tf_op jit(solution)/shard_map/slice | solution.py:317
  1.2 1.3 %copy.18 = f32[5,16,9,360]{3,1,0,2:T(8,128)S(1)} copy(f32[5,16,9,360]{3,1,2,0:T(8,128)} %param.5) | data formatting | bytes 2073600 | tf_op args[0]
  2.5 0.5 slice_reduce_fusion
  3.2 5.1 %collective-permute-start.3 = (f32[96,9]{1,0:T(8,128)S(1)}, f32[96,9]{1,0:T(8,128)}, u32[]{:S(2)}, u32[]{:S(2)}) collective-permute-start(f32[96,9]{1,0:T(8,128)S(1)} %copy.22), channel_id=1, source_target_pairs={{0,3},{1,0},{2,1},{3,2},{4,7},{5,4},{6,5},{7,6},{8,11},{9,8},{10,9... | collective-permute-start | bytes 10376 | tf_op jit(solution)/shard_map/ppermute | solution.py:319
  8.5 0.7 copy.20
  9.3 0.8 slice_bitcast_fusion.3
  10.1 0.7 fusion.17
  10.8 1.0 %collective-permute-start = (f32[96,360]{1,0:T(8,128)}, f32[96,360]{1,0:T(8,128)}, u32[]{:S(2)}, u32[]{:S(2)}) collective-permute-start(f32[96,360]{1,0:T(8,128)} %get-tuple-element.46), channel_id=1, source_target_pairs={{0,2},{1,3},{2,0},{3,1},{28,30},{29,31},{30,28},{31,29},{4,8},{8,4... | collective-permute-start | bytes 414728 | tf_op jit(solution)/shard_map/ppermute | solution.py:305
  11.8 3.5 %shard_map.56 = (f32[120,384]{1,0:T(8,128)}, f32[120,384]{1,0:T(8,128)}, f32[120,384]{1,0:T(8,128)}, f32[120,384]{1,0:T(8,128)}) custom-call(f32[9,80,360]{2,1,0:T(8,128)} %bitcast.26, f32[9,16,360]{2,1,0:T(8,128)} %bitcast.29, f32[9,16,360]{2,1,0:T(8,128)} %bitcast.32), custom_call_target="tpu_custom_call" | custom-call | tf_op jit(solution)/shard_map/pallas_call | solution.py:307
  15.4 4.7 %collective-permute-start.4 = (f32[120,384]{1,0:T(8,128)}, f32[120,384]{1,0:T(8,128)S(1)}, u32[]{:S(2)}, u32[]{:S(2)}) collective-permute-start(f32[120,384]{1,0:T(8,128)} %get-tuple-element.24), channel_id=1, source_target_pairs={{0,3},{1,0},{2,1},{3,2},{28,31},{29,28},{30,29},{31,30}} | collective-permute-start | bytes 552968 | tf_op jit(solution)/shard_map/ppermute | solution.py:313
  20.2 1.6 %fusion.8 = (f32[6,40,360]{2,1,0:T(8,128)S(1)}, f32[6,40,360]{2,1,0:T(8,128)S(1)}) fusion(s32[6,360]{1,0:T(8,128)S(1)} %stack.2), kind=kLoop, calls=%fused_computation.16 | loop fusion | flops 950400 | bytes 699840 | tf_op jit(solution)/shard_map/add | solution.py:268
  21.7 0.7 fusion.15
  22.9 3.9 %collective-permute-start.5 = (f32[120,384]{1,0:T(8,128)}, f32[120,384]{1,0:T(8,128)}, u32[]{:S(2)}, u32[]{:S(2)}) collective-permute-start(f32[120,384]{1,0:T(8,128)} %get-tuple-element.25), channel_id=1, source_target_pairs={{0,2},{1,3},{2,0},{3,1},{28,30},{29,31},{30,28},{31,29}} | collective-permute-start | bytes 552968 | tf_op jit(solution)/shard_map/ppermute | solution.py:313
  26.8 1.9 %collective-permute-start.6 = (f32[120,384]{1,0:T(8,128)}, f32[120,384]{1,0:T(8,128)}, u32[]{:S(2)}, u32[]{:S(2)}) collective-permute-start(f32[120,384]{1,0:T(8,128)} %get-tuple-element.26), channel_id=1, source_target_pairs={{0,1},{1,2},{2,3},{3,0},{28,29},{29,30},{30,31},{31,28}} | collective-permute-start | bytes 552968 | tf_op jit(solution)/shard_map/ppermute | solution.py:313
  28.8 4.6 %shard_map.55 = (f32[60,384]{1,0:T(8,128)}, f32[60,384]{1,0:T(8,128)}, f32[60,384]{1,0:T(8,128)}, f32[60,384]{1,0:T(8,128)}, f32[9,80,360]{2,1,0:T(8,128)}) custom-call(f32[9,80,360]{2,1,0:T(8,128)} %bitcast.27, f32[9,16,360]{2,1,0:T(8,128)} %bitcast.30, f32[9,16,360]{2,1,0:T(8,128)} %bitcast.33, f32[96,360]{1,0:T(8,128)} %collective-permute-done.refs_3_, ...), custom_call_target="tpu_custom_call" | custom-call | tf_op jit(solution)/shard_map/pallas_call | solution.py:321
  33.4 5.7 %collective-permute-start.10 = (f32[60,384]{1,0:T(8,128)}, f32[60,384]{1,0:T(8,128)}, u32[]{:S(2)}, u32[]{:S(2)}) collective-permute-start(f32[60,384]{1,0:T(8,128)} %get-tuple-element.32), channel_id=1, source_target_pairs={{0,3},{1,0},{2,1},{3,2},{4,7},{5,4},{6,5},{7,6},{24,27},{25,24},{2... | collective-permute-start | bytes 276488 | tf_op jit(solution)/shard_map/ppermute | solution.py:327
  39.1 1.9 %collective-permute-start.11 = (f32[60,384]{1,0:T(8,128)}, f32[60,384]{1,0:T(8,128)}, u32[]{:S(2)}, u32[]{:S(2)}) collective-permute-start(f32[60,384]{1,0:T(8,128)} %get-tuple-element.33), channel_id=1, source_target_pairs={{0,2},{1,3},{2,0},{3,1},{4,6},{5,7},{6,4},{7,5},{24,26},{25,27},{2... | collective-permute-start | bytes 276488 | tf_op jit(solution)/shard_map/ppermute | solution.py:327
  41.1 2.7 %collective-permute-start.12 = (f32[60,384]{1,0:T(8,128)}, f32[60,384]{1,0:T(8,128)}, u32[]{:S(2)}, u32[]{:S(2)}) collective-permute-start(f32[60,384]{1,0:T(8,128)} %get-tuple-element.34), channel_id=1, source_target_pairs={{0,1},{1,2},{2,3},{3,0},{4,5},{5,6},{6,7},{7,4},{24,25},{25,26},{2... | collective-permute-start | bytes 276488 | tf_op jit(solution)/shard_map/ppermute | solution.py:327
  43.8 2.4 %fusion = (bf16[6,360,360]{2,1,0:T(8,128)(2,1)}, bf16[6,360,360]{2,1,0:T(8,128)(2,1)}) fusion(f32[6,9,40,360]{3,2,1,0:T(8,128)S(1)} %multiply_add_fusion, f32[6]{0:T(128)S(1)} %copy-done.8), kind=kLoop, calls=%fused_computation.2 | loop fusion | flops 3888000 | bytes 6220824 | tf_op jit(solution)/shard_map/convert_element_type | solution.py:271
  46.2 5.9 %shard_map.57 = (f32[120,360]{1,0:T(8,128)}, f32[120,360]{1,0:T(8,128)}, f32[120,360]{1,0:T(8,128)}, f32[120,360]{1,0:T(8,128)}) custom-call(s32[9]{0:T(128)} %refs_0_.3, bf16[6,360,360]{2,1,0:T(8,128)(2,1)} %get-tuple-element.42.refs_1_, bf16[6,360,360]{2,1,0:T(8,128)(2,1)} %get-tuple-element.41.refs_2_, f32[120,384]{1,0:T(8,128)} %get-tuple-element.23.refs_3_, ...), custom_call_target="tpu_custom_call" | custom-call | tf_op jit(solution)/shard_map/pallas_call | solution.py:336
  52.1 4.6 %shard_map.58 = (f32[60,360]{1,0:T(8,128)}, f32[60,360]{1,0:T(8,128)}, f32[60,360]{1,0:T(8,128)}, f32[60,360]{1,0:T(8,128)}) custom-call(s32[9]{0:T(128)} %refs_0_.3, bf16[6,360,360]{2,1,0:T(8,128)(2,1)} %get-tuple-element.42.refs_1_, bf16[6,360,360]{2,1,0:T(8,128)(2,1)} %get-tuple-element.41.refs_2_, f32[60,384]{1,0:T(8,128)} %get-tuple-element.31.refs_3_, ...), custom_call_target="tpu_custom_call" | custom-call | tf_op jit(solution)/shard_map/pallas_call | solution.py:336
  56.7 4.8 %collective-permute-start.13 = (f32[60,360]{1,0:T(8,128)}, f32[60,360]{1,0:T(8,128)S(1)}, u32[]{:S(2)}, u32[]{:S(2)}) collective-permute-start(f32[60,360]{1,0:T(8,128)} %get-tuple-element.36), channel_id=1, source_target_pairs={{0,1},{1,2},{2,3},{3,0},{4,5},{5,6},{6,7},{7,4},{24,25},{25,26},{2... | collective-permute-start | bytes 259208 | tf_op jit(solution)/shard_map/ppermute | solution.py:342
  61.5 1.9 %collective-permute-start.7 = (f32[120,360]{1,0:T(8,128)S(1)}, f32[120,360]{1,0:T(8,128)S(1)}, u32[]{:S(2)}, u32[]{:S(2)}) collective-permute-start(f32[120,360]{1,0:T(8,128)S(1)} %copy-done.11), channel_id=1, source_target_pairs={{0,1},{1,2},{2,3},{3,0},{28,29},{29,30},{30,31},{31,28}} | collective-permute-start | bytes 518408 | tf_op jit(solution)/shard_map/ppermute | solution.py:342
  63.5 3.4 %collective-permute-start.8 = (f32[120,360]{1,0:T(8,128)S(1)}, f32[120,360]{1,0:T(8,128)S(1)}, u32[]{:S(2)}, u32[]{:S(2)}) collective-permute-start(f32[120,360]{1,0:T(8,128)S(1)} %copy-done.10), channel_id=1, source_target_pairs={{0,2},{1,3},{2,0},{3,1},{28,30},{29,31},{30,28},{31,29}} | collective-permute-start | bytes 518408 | tf_op jit(solution)/shard_map/ppermute | solution.py:342
  66.9 4.3 %collective-permute-start.9 = (f32[120,360]{1,0:T(8,128)S(1)}, f32[120,360]{1,0:T(8,128)S(1)}, u32[]{:S(2)}, u32[]{:S(2)}) collective-permute-start(f32[120,360]{1,0:T(8,128)S(1)} %copy-done.9), channel_id=1, source_target_pairs={{0,3},{1,0},{2,1},{3,2},{28,31},{29,28},{30,29},{31,30}} | collective-permute-start | bytes 518408 | tf_op jit(solution)/shard_map/ppermute | solution.py:342
  71.2 3.9 %collective-permute-start.14 = (f32[60,360]{1,0:T(8,128)}, f32[60,360]{1,0:T(8,128)S(1)}, u32[]{:S(2)}, u32[]{:S(2)}) collective-permute-start(f32[60,360]{1,0:T(8,128)} %get-tuple-element.37), channel_id=1, source_target_pairs={{0,2},{1,3},{2,0},{3,1},{4,6},{5,7},{6,4},{7,5},{24,26},{25,27},{2... | collective-permute-start | bytes 259208 | tf_op jit(solution)/shard_map/ppermute | solution.py:342
  75.1 2.8 %collective-permute-start.15 = (f32[60,360]{1,0:T(8,128)}, f32[60,360]{1,0:T(8,128)S(1)}, u32[]{:S(2)}, u32[]{:S(2)}) collective-permute-start(f32[60,360]{1,0:T(8,128)} %get-tuple-element.38), channel_id=1, source_target_pairs={{0,3},{1,0},{2,1},{3,2},{4,7},{5,4},{6,5},{7,6},{24,27},{25,24},{2... | collective-permute-start | bytes 259208 | tf_op jit(solution)/shard_map/ppermute | solution.py:342
  77.9 1.9 %collective-permute-done.14.refs_7_ = f32[60,360]{1,0:T(8,128)S(1)} collective-permute-done((f32[60,360]{1,0:T(8,128)}, f32[60,360]{1,0:T(8,128)S(1)}, u32[]{:S(2)}, u32[]{:S(2)}) %collective-permute-start.14) | collective-permute-done | bytes 86432 | tf_op jit(solution)/shard_map/ppermute | solution.py:342
  79.8 2.0 %collective-permute-done.15.refs_8_ = f32[60,360]{1,0:T(8,128)S(1)} collective-permute-done((f32[60,360]{1,0:T(8,128)}, f32[60,360]{1,0:T(8,128)S(1)}, u32[]{:S(2)}, u32[]{:S(2)}) %collective-permute-start.15) | collective-permute-done | bytes 86432 | tf_op jit(solution)/shard_map/ppermute | solution.py:342
  81.9 0.6 copy-done.7
  82.6 2.8 %shard_map.59 = f32[9,80,360]{2,1,0:T(8,128)} custom-call(f32[9,80,360]{2,1,0:T(8,128)} %get-tuple-element.22.refs_0_, f32[120,360]{1,0:T(8,128)} %get-tuple-element.27.refs_1_, f32[120,360]{1,0:T(8,128)} %copy-done.1, f32[120,360]{1,0:T(8,128)} %copy-done.2, f32[120,360]{1,0:T(8,128)} %copy-done.3, f32[60,360]{1,0:T(8,128)} %get-tuple-element.35.refs_5_, ...), custom_call_target="tpu_custom_call" | custom-call | tf_op jit(solution)/shard_map/pallas_call | solution.py:347
  85.4 2.3 %copy.23 = f32[5,16,9,360]{3,1,2,0:T(8,128)} copy(f32[5,16,9,360]{3,1,0,2:T(8,128)} %bitcast.28) | data formatting | bytes 2073600 | tf_op jit(solution)/shard_map/reshape | solution.py:352
  (51 shorter events, 1.3 us)
Async XLA Ops:
  2.5 9.3 %copy-start = (f32[5,16,9,360]{3,1,0,2:T(8,128)}, f32[5,16,9,360]{3,1,0,2:T(8,128)S(1)}, u32[]{:S(2)}) copy-start(f32[5,16,9,360]{3,1,0,2:T(8,128)S(1)} %copy.18) | copy-start | bytes 3110404
  3.2 19.7 %collective-permute-start.3 = (f32[96,9]{1,0:T(8,128)S(1)}, f32[96,9]{1,0:T(8,128)}, u32[]{:S(2)}, u32[]{:S(2)}) collective-permute-start(f32[96,9]{1,0:T(8,128)S(1)} %copy.22), channel_id=1, source_target_pairs={{0,3},{1,0},{2,1},{3,2},{4,7},{5,4},{6,5},{7,6},{8,11},{9,8},{10,9... | collective-permute-start | bytes 10376 | tf_op jit(solution)/shard_map/ppermute | solution.py:319
  9.3 17.5 %collective-permute-start.2 = (f32[96,9]{1,0:T(8,128)}, f32[96,9]{1,0:T(8,128)}, u32[]{:S(2)}, u32[]{:S(2)}) collective-permute-start(f32[96,9]{1,0:T(8,128)} %copy.20), channel_id=1, source_target_pairs={{0,1},{1,2},{2,3},{3,0},{4,5},{5,6},{6,7},{7,4},{8,9},{9,10},{10,1... | collective-permute-start | bytes 10376 | tf_op jit(solution)/shard_map/ppermute | solution.py:318
  10.8 18.0 %collective-permute-start.1 = (f32[96,360]{1,0:T(8,128)}, f32[96,360]{1,0:T(8,128)}, u32[]{:S(2)}, u32[]{:S(2)}) collective-permute-start(f32[96,360]{1,0:T(8,128)} %get-tuple-element.45), channel_id=1, source_target_pairs={{0,4},{1,5},{2,6},{3,7},{4,0},{5,1},{6,2},{7,3},{8,12},{9,13},{10,... | collective-permute-start | bytes 414728 | tf_op jit(solution)/shard_map/ppermute | solution.py:304
  10.8 18.0 %collective-permute-start = (f32[96,360]{1,0:T(8,128)}, f32[96,360]{1,0:T(8,128)}, u32[]{:S(2)}, u32[]{:S(2)}) collective-permute-start(f32[96,360]{1,0:T(8,128)} %get-tuple-element.46), channel_id=1, source_target_pairs={{0,2},{1,3},{2,0},{3,1},{28,30},{29,31},{30,28},{31,29},{4,8},{8,4... | collective-permute-start | bytes 414728 | tf_op jit(solution)/shard_map/ppermute | solution.py:305
  15.4 25.7 %collective-permute-start.4 = (f32[120,384]{1,0:T(8,128)}, f32[120,384]{1,0:T(8,128)S(1)}, u32[]{:S(2)}, u32[]{:S(2)}) collective-permute-start(f32[120,384]{1,0:T(8,128)} %get-tuple-element.24), channel_id=1, source_target_pairs={{0,3},{1,0},{2,1},{3,2},{28,31},{29,28},{30,29},{31,30}} | collective-permute-start | bytes 552968 | tf_op jit(solution)/shard_map/ppermute | solution.py:313
  21.7 22.0 %copy-start.8 = (f32[6]{0:T(128)S(1)}, f32[6]{0:T(128)}, u32[]{:S(2)}) copy-start(f32[6]{0:T(128)} %constant.43.clone) | copy-start | bytes 76
  22.9 23.3 %collective-permute-start.5 = (f32[120,384]{1,0:T(8,128)}, f32[120,384]{1,0:T(8,128)}, u32[]{:S(2)}, u32[]{:S(2)}) collective-permute-start(f32[120,384]{1,0:T(8,128)} %get-tuple-element.25), channel_id=1, source_target_pairs={{0,2},{1,3},{2,0},{3,1},{28,30},{29,31},{30,28},{31,29}} | collective-permute-start | bytes 552968 | tf_op jit(solution)/shard_map/ppermute | solution.py:313
  26.8 19.4 %collective-permute-start.6 = (f32[120,384]{1,0:T(8,128)}, f32[120,384]{1,0:T(8,128)}, u32[]{:S(2)}, u32[]{:S(2)}) collective-permute-start(f32[120,384]{1,0:T(8,128)} %get-tuple-element.26), channel_id=1, source_target_pairs={{0,1},{1,2},{2,3},{3,0},{28,29},{29,30},{30,31},{31,28}} | collective-permute-start | bytes 552968 | tf_op jit(solution)/shard_map/ppermute | solution.py:313
  33.4 18.6 %collective-permute-start.10 = (f32[60,384]{1,0:T(8,128)}, f32[60,384]{1,0:T(8,128)}, u32[]{:S(2)}, u32[]{:S(2)}) collective-permute-start(f32[60,384]{1,0:T(8,128)} %get-tuple-element.32), channel_id=1, source_target_pairs={{0,3},{1,0},{2,1},{3,2},{4,7},{5,4},{6,5},{7,6},{24,27},{25,24},{2... | collective-permute-start | bytes 276488 | tf_op jit(solution)/shard_map/ppermute | solution.py:327
  39.1 12.9 %collective-permute-start.11 = (f32[60,384]{1,0:T(8,128)}, f32[60,384]{1,0:T(8,128)}, u32[]{:S(2)}, u32[]{:S(2)}) collective-permute-start(f32[60,384]{1,0:T(8,128)} %get-tuple-element.33), channel_id=1, source_target_pairs={{0,2},{1,3},{2,0},{3,1},{4,6},{5,7},{6,4},{7,5},{24,26},{25,27},{2... | collective-permute-start | bytes 276488 | tf_op jit(solution)/shard_map/ppermute | solution.py:327
  41.1 5.1 %copy-start.4 = (f32[120,384]{1,0:T(8,128)}, f32[120,384]{1,0:T(8,128)S(1)}, u32[]{:S(2)}) copy-start(f32[120,384]{1,0:T(8,128)S(1)} %collective-permute-done.4.refs_4_) | copy-start | bytes 552964
  41.1 11.0 %collective-permute-start.12 = (f32[60,384]{1,0:T(8,128)}, f32[60,384]{1,0:T(8,128)}, u32[]{:S(2)}, u32[]{:S(2)}) collective-permute-start(f32[60,384]{1,0:T(8,128)} %get-tuple-element.34), channel_id=1, source_target_pairs={{0,1},{1,2},{2,3},{3,0},{4,5},{5,6},{6,7},{7,4},{24,25},{25,26},{2... | collective-permute-start | bytes 276488 | tf_op jit(solution)/shard_map/ppermute | solution.py:327
  52.0 9.5 %copy-start.11 = (f32[120,360]{1,0:T(8,128)S(1)}, f32[120,360]{1,0:T(8,128)}, u32[]{:S(2)}) copy-start(f32[120,360]{1,0:T(8,128)} %get-tuple-element.28) | copy-start | bytes 518404
  52.0 11.4 %copy-start.10 = (f32[120,360]{1,0:T(8,128)S(1)}, f32[120,360]{1,0:T(8,128)}, u32[]{:S(2)}) copy-start(f32[120,360]{1,0:T(8,128)} %get-tuple-element.29) | copy-start | bytes 518404
  52.1 14.8 %copy-start.9 = (f32[120,360]{1,0:T(8,128)S(1)}, f32[120,360]{1,0:T(8,128)}, u32[]{:S(2)}) copy-start(f32[120,360]{1,0:T(8,128)} %get-tuple-element.30) | copy-start | bytes 518404
  56.7 18.4 %collective-permute-start.13 = (f32[60,360]{1,0:T(8,128)}, f32[60,360]{1,0:T(8,128)S(1)}, u32[]{:S(2)}, u32[]{:S(2)}) collective-permute-start(f32[60,360]{1,0:T(8,128)} %get-tuple-element.36), channel_id=1, source_target_pairs={{0,1},{1,2},{2,3},{3,0},{4,5},{5,6},{6,7},{7,4},{24,25},{25,26},{2... | collective-permute-start | bytes 259208 | tf_op jit(solution)/shard_map/ppermute | solution.py:342
  61.5 20.3 %collective-permute-start.7 = (f32[120,360]{1,0:T(8,128)S(1)}, f32[120,360]{1,0:T(8,128)S(1)}, u32[]{:S(2)}, u32[]{:S(2)}) collective-permute-start(f32[120,360]{1,0:T(8,128)S(1)} %copy-done.11), channel_id=1, source_target_pairs={{0,1},{1,2},{2,3},{3,0},{28,29},{29,30},{30,31},{31,28}} | collective-permute-start | bytes 518408 | tf_op jit(solution)/shard_map/ppermute | solution.py:342
  63.5 18.3 %collective-permute-start.8 = (f32[120,360]{1,0:T(8,128)S(1)}, f32[120,360]{1,0:T(8,128)S(1)}, u32[]{:S(2)}, u32[]{:S(2)}) collective-permute-start(f32[120,360]{1,0:T(8,128)S(1)} %copy-done.10), channel_id=1, source_target_pairs={{0,2},{1,3},{2,0},{3,1},{28,30},{29,31},{30,28},{31,29}} | collective-permute-start | bytes 518408 | tf_op jit(solution)/shard_map/ppermute | solution.py:342
  66.9 15.0 %collective-permute-start.9 = (f32[120,360]{1,0:T(8,128)S(1)}, f32[120,360]{1,0:T(8,128)S(1)}, u32[]{:S(2)}, u32[]{:S(2)}) collective-permute-start(f32[120,360]{1,0:T(8,128)S(1)} %copy-done.9), channel_id=1, source_target_pairs={{0,3},{1,0},{2,1},{3,2},{28,31},{29,28},{30,29},{31,30}} | collective-permute-start | bytes 518408 | tf_op jit(solution)/shard_map/ppermute | solution.py:342
  71.2 8.7 %collective-permute-start.14 = (f32[60,360]{1,0:T(8,128)}, f32[60,360]{1,0:T(8,128)S(1)}, u32[]{:S(2)}, u32[]{:S(2)}) collective-permute-start(f32[60,360]{1,0:T(8,128)} %get-tuple-element.37), channel_id=1, source_target_pairs={{0,2},{1,3},{2,0},{3,1},{4,6},{5,7},{6,4},{7,5},{24,26},{25,27},{2... | collective-permute-start | bytes 259208 | tf_op jit(solution)/shard_map/ppermute | solution.py:342
  75.1 6.8 %copy-start.5 = (f32[60,360]{1,0:T(8,128)}, f32[60,360]{1,0:T(8,128)S(1)}, u32[]{:S(2)}) copy-start(f32[60,360]{1,0:T(8,128)S(1)} %collective-permute-done.13.refs_6_) | copy-start | bytes 259204
  75.1 6.7 %collective-permute-start.15 = (f32[60,360]{1,0:T(8,128)}, f32[60,360]{1,0:T(8,128)S(1)}, u32[]{:S(2)}, u32[]{:S(2)}) collective-permute-start(f32[60,360]{1,0:T(8,128)} %get-tuple-element.38), channel_id=1, source_target_pairs={{0,3},{1,0},{2,1},{3,2},{4,7},{5,4},{6,5},{7,6},{24,27},{25,24},{2... | collective-permute-start | bytes 259208 | tf_op jit(solution)/shard_map/ppermute | solution.py:342
  79.8 2.1 %copy-start.6 = (f32[60,360]{1,0:T(8,128)}, f32[60,360]{1,0:T(8,128)S(1)}, u32[]{:S(2)}) copy-start(f32[60,360]{1,0:T(8,128)S(1)} %collective-permute-done.14.refs_7_) | copy-start | bytes 259204
  81.8 0.6 copy-start.7
  81.8 0.7 copy-start.1
  81.8 0.8 copy-start.2
  81.8 0.8 copy-start.3

commit v2 on v1

--- a/solution.py
+++ b/solution.py
@@ -287,8 +287,16 @@
     def shift_pairs(lats, by):
         return [(device(a, z), device(a, z + by)) for a in lats for z in range(n_lon)]
 
-    full_lats = list(range(plan.full)) + list(range(n_lat - plan.full, n_lat))
-    polar_lats = list(range(plan.full + 1)) + list(range(n_lat - plan.full - 1, n_lat))
+    def x_pairs(by):
+        return shift_pairs(range(n_lat), by)
+
+    def y_pairs(by):
+        spare = list(range(plan.full + 1, n_lat - plan.full - 1))
+        swaps = [(plan.full, n_lat - 1 - plan.full)] + list(zip(spare[0::2], spare[1::2]))
+        pairs = shift_pairs(list(range(plan.full)) + list(range(n_lat - plan.full, n_lat)), by)
+        for a, b in swaps:
+            pairs += [(device(p, z), device(q, z)) for p, q in ((a, b), (b, a)) for z in range(n_lon)]
+        return pairs
 
     qt, ut, vt = (jnp.transpose(x, (1, 0, 2)) for x in (q, u, v))
 
@@ -310,7 +318,7 @@
         [(n_lon, plan.y_count, width), (planes, width), (levels, width)],
     )(qt, ut, vt)
     y_got = [y_send[0]] + [
-        lax.ppermute(y_send[s], both, shift_pairs(full_lats, s)) for s in range(1, n_lon)
+        lax.ppermute(y_send[s], both, y_pairs(s)) for s in range(1, n_lon)
     ]
 
     last = jnp.concatenate([q[:, :, -1], u[:, :, -1]], axis=0)
@@ -324,14 +332,14 @@
         [(n_lon, plan.x_count, width), (planes, width), (levels, width), (rows, planes, width)],
     )(qt, ut, vt, one, two, west, east)
     x_got = [x_send[0]] + [
-        lax.ppermute(x_send[s], both, shift_pairs(polar_lats, s)) for s in range(1, n_lon)
+        lax.ppermute(x_send[s], both, x_pairs(s)) for s in range(1, n_lon)
     ]
 
     hi, lo = transform_tables(plan)
     vmem = pl.BlockSpec(memory_space=pltpu.VMEM)
     smem = pl.BlockSpec(memory_space=pltpu.SMEM)
 
-    def filtered(got, count, row_of, with_edges, lats):
+    def filtered(got, count, row_of, with_edges, pairs):
         ordered = [got[(n_lon - j) % n_lon] for j in range(n_lon)]
         pieces = call(
             lambda *refs: filter_kernel(plan, count, row_of, with_edges, *refs),
@@ -339,11 +347,11 @@
             in_specs=[smem] + [vmem] * (2 + n_lon),
         )(cutoff, hi, lo, *ordered)
         return [pieces[0]] + [
-            lax.ppermute(pieces[s], both, shift_pairs(lats, s)) for s in range(1, n_lon)
+            lax.ppermute(pieces[s], both, pairs(s)) for s in range(1, n_lon)
         ]
 
-    y_back = filtered(y_got, plan.y_count, lambda i, lat: 1 + i, True, full_lats)
-    x_back = filtered(x_got, plan.x_count, plan.x_row, False, polar_lats)
+    y_back = filtered(y_got, plan.y_count, lambda i, lat: 1 + i, True, y_pairs)
+    x_back = filtered(x_got, plan.x_count, plan.x_row, False, x_pairs)
     (merged,) = call(
         lambda *refs: merge_kernel(plan, *refs),
         [(rows, planes, sector)],

time: 88.5 us -> 72.2 us (0.82)
  starting transfers between devices: 48.1 us -> 24.7 us
  waiting for transfers between devices: 3.93 us -> 11.6 us
    ppermute x12, starting transfers between devices: 41.9 us -> 18.5 us  [the longest x6 9.26 us: filtered(): lax.ppermute(pieces[s], both, pairs(s))]
    ppermute x12, waiting for transfers between devices: 3.92 us -> 11.6 us  [the longest x6 11.1 us: filtered(): lax.ppermute(pieces[s], both, pairs(s))]
  transfers between devices with their start and end apart: 16 -> 16, of which waited for: 2 -> 2; matrix products, arithmetic and copies ran while one was open for 9% -> 11% of each run, Pallas kernels for 16% -> 20%
where the time goes in v2:
time: 72.2 us; the launch traced here: 71.8 us
  starting transfers between devices  24.7 us (34%)
  Pallas kernels  21.4 us (30%)
  waiting for transfers between devices  11.6 us (16%)
  local copies, waits for them, and re-layouts  7.9 us (11%)
  other arithmetic  6.02 us (8%)
    ppermute x6, waiting for transfers between devices, filtered(): lax.ppermute(pieces[s], both, pairs(s))  11.1 us
    pallas_call x2, Pallas kernels, filtered(): call(lambda *refs: filter_kernel(plan, count, row_of, with_edges, *refs),...  10.4 us
    ppermute x6, starting transfers between devices, filtered(): lax.ppermute(pieces[s], both, pairs(s))  9.26 us
    ppermute x1, starting transfers between devices, body(): lax.ppermute(first, 'lon', [(i, (i - 1) % n_lon) for i in range(n_lon)])  5.13 us
    ppermute x3, starting transfers between devices, body(): lax.ppermute(y_send[s], both, y_pairs(s))  4.9 us
    pallas_call x1, Pallas kernels, body(): call(lambda *refs: all_rows_kernel(plan, *refs), [(plan.x_count, width)]...  4.65 us
    ppermute x3, starting transfers between devices, body(): lax.ppermute(x_send[s], both, x_pairs(s))  4.37 us
    pallas_call x1, Pallas kernels, body(): call(lambda *refs: inner_rows_kernel(plan, *refs), [(plan.y_count, width)...  3.54 us
  transfers between devices with their start and end apart: 16, of which 2 were waited for; matrix products, arithmetic and copies ran while one was open for 11% of the time, Pallas kernels for 20%

profile of v2, /device:TPU:0, one launch (start us, length us, event | category | flops | bytes accessed | tf_op | source)
XLA Modules:
  0.0 71.8 jit_solution(1313162203277961405)
XLA Ops:
  0.0 1.0 %fusion.21 = (f32[16,9,1]{2,0,1:T(8,128)S(1)}, f32[16,9,1]{2,0,1:T(8,128)S(1)}) fusion(f32[16,9,360]{2,0,1:T(8,128)} %param.6), kind=kLoop, calls=%fused_computation.44 | loop fusion | bytes 2304 | tf_op jit(solution)/shard_map/slice | solution.py:325
  1.0 0.1 copy.25
  1.2 1.3 %copy.18 = f32[5,16,9,360]{3,1,0,2:T(8,128)S(1)} copy(f32[5,16,9,360]{3,1,2,0:T(8,128)} %param.5) | data formatting | bytes 2073600 | tf_op args[0]
  2.5 0.5 slice_reduce_fusion
  3.2 5.1 %collective-permute-start.3 = (f32[96,9]{1,0:T(8,128)S(1)}, f32[96,9]{1,0:T(8,128)}, u32[]{:S(2)}, u32[]{:S(2)}) collective-permute-start(f32[96,9]{1,0:T(8,128)S(1)} %copy.22), channel_id=1, source_target_pairs={{0,3},{1,0},{2,1},{3,2},{4,7},{5,4},{6,5},{7,6},{8,11},{9,8},{10,9... | collective-permute-start | bytes 10376 | tf_op jit(solution)/shard_map/ppermute | solution.py:327
  8.5 0.7 %copy.20 = f32[96,9]{1,0:T(8,128)} copy(f32[96,9]{0,1:T(8,128)S(1)} %pad_maximum_fusion.2) | data formatting | bytes 6912 | tf_op jit(solution)/shard_map/concatenate | solution.py:324
  9.3 0.8 %slice_bitcast_fusion.3 = (f32[16,360]{1,0:T(8,128)S(1)}, f32[16,360]{1,0:T(8,128)S(1)}) fusion(f32[9,16,360]{2,1,0:T(8,128)} %bitcast.31), kind=kLoop, calls=%fused_computation.34 | loop fusion | bytes 92160 | tf_op jit(solution)/shard_map/squeeze | solution.py:304
  10.1 0.7 %fusion.17 = (f32[96,360]{1,0:T(8,128)}, f32[96,360]{1,0:T(8,128)}) fusion(f32[16,360]{1,0:T(8,128)S(1)} %get-tuple-element.50, f32[80,360]{1,0:T(8,128)S(1)} %get-tuple-element.44, f32[16,360]{1,0:T(8,128)S(1)} %get-tuple-element.49, f32[80,360]{1,0:T(8,128)S(1)} %get-tuple-element.43, pred[]{:T(512)S(6)} %eq.8), kind=kLoop, calls=%fused_computation.31 | loop fusion | flops 138240 | bytes 552961 | tf_op jit(solution)/shard_map/jit(_where)/select_n | solution.py:306
  10.8 1.0 %collective-permute-start = (f32[96,360]{1,0:T(8,128)}, f32[96,360]{1,0:T(8,128)}, u32[]{:S(2)}, u32[]{:S(2)}) collective-permute-start(f32[96,360]{1,0:T(8,128)} %get-tuple-element.46), channel_id=1, source_target_pairs={{0,2},{1,3},{2,0},{3,1},{28,30},{29,31},{30,28},{31,29},{4,8},{8,4... | collective-permute-start | bytes 414728 | tf_op jit(solution)/shard_map/ppermute | solution.py:313
  11.8 3.5 %shard_map.56 = (f32[120,384]{1,0:T(8,128)}, f32[120,384]{1,0:T(8,128)}, f32[120,384]{1,0:T(8,128)}, f32[120,384]{1,0:T(8,128)}) custom-call(f32[9,80,360]{2,1,0:T(8,128)} %bitcast.26, f32[9,16,360]{2,1,0:T(8,128)} %bitcast.29, f32[9,16,360]{2,1,0:T(8,128)} %bitcast.32), custom_call_target="tpu_custom_call" | custom-call | tf_op jit(solution)/shard_map/pallas_call | solution.py:315
  15.4 2.8 %collective-permute-start.4 = (f32[120,384]{1,0:T(8,128)}, f32[120,384]{1,0:T(8,128)S(1)}, u32[]{:S(2)}, u32[]{:S(2)}) collective-permute-start(f32[120,384]{1,0:T(8,128)} %get-tuple-element.24), channel_id=1, source_target_pairs={{0,3},{1,0},{2,1},{3,2},{28,31},{29,28},{30,29},{31,30},{4,24},{5,... | collective-permute-start | bytes 552968 | tf_op jit(solution)/shard_map/ppermute | solution.py:321
  18.3 1.6 %fusion.8 = (f32[6,40,360]{2,1,0:T(8,128)S(1)}, f32[6,40,360]{2,1,0:T(8,128)S(1)}) fusion(s32[6,360]{1,0:T(8,128)S(1)} %stack.2), kind=kLoop, calls=%fused_computation.16 | loop fusion | flops 950400 | bytes 699840 | tf_op jit(solution)/shard_map/add | solution.py:268
  19.8 0.7 fusion.15
  20.5 0.4 multiply_add_fusion
  21.0 2.1 %collective-permute-start.5 = (f32[120,384]{1,0:T(8,128)}, f32[120,384]{1,0:T(8,128)}, u32[]{:S(2)}, u32[]{:S(2)}) collective-permute-start(f32[120,384]{1,0:T(8,128)} %get-tuple-element.25), channel_id=1, source_target_pairs={{0,2},{1,3},{2,0},{3,1},{28,30},{29,31},{30,28},{31,29},{4,24},{5,... | collective-permute-start | bytes 552968 | tf_op jit(solution)/shard_map/ppermute | solution.py:321
  23.1 4.6 %shard_map.55 = (f32[60,384]{1,0:T(8,128)}, f32[60,384]{1,0:T(8,128)}, f32[60,384]{1,0:T(8,128)}, f32[60,384]{1,0:T(8,128)}, f32[9,80,360]{2,1,0:T(8,128)}) custom-call(f32[9,80,360]{2,1,0:T(8,128)} %bitcast.27, f32[9,16,360]{2,1,0:T(8,128)} %bitcast.30, f32[9,16,360]{2,1,0:T(8,128)} %bitcast.33, f32[96,360]{1,0:T(8,128)} %collective-permute-done.refs_3_, ...), custom_call_target="tpu_custom_call" | custom-call | tf_op jit(solution)/shard_map/pallas_call | solution.py:329
  27.7 3.8 %collective-permute-start.10 = (f32[60,384]{1,0:T(8,128)}, f32[60,384]{1,0:T(8,128)}, u32[]{:S(2)}, u32[]{:S(2)}) collective-permute-start(f32[60,384]{1,0:T(8,128)} %get-tuple-element.32), channel_id=1, source_target_pairs={{0,3},{1,0},{2,1},{3,2},{4,7},{5,4},{6,5},{7,6},{8,11},{9,8},{10,9... | collective-permute-start | bytes 276488 | tf_op jit(solution)/shard_map/ppermute | solution.py:335
  31.5 0.6 collective-permute-start.12
  32.1 2.4 %fusion = (bf16[6,360,360]{2,1,0:T(8,128)(2,1)}, bf16[6,360,360]{2,1,0:T(8,128)(2,1)}) fusion(f32[6,9,40,360]{3,2,1,0:T(8,128)S(1)} %multiply_add_fusion, f32[6]{0:T(128)S(1)} %copy-done.8), kind=kLoop, calls=%fused_computation.2 | loop fusion | flops 3888000 | bytes 6220824 | tf_op jit(solution)/shard_map/convert_element_type | solution.py:271
  34.5 5.9 %shard_map.57 = (f32[120,360]{1,0:T(8,128)}, f32[120,360]{1,0:T(8,128)}, f32[120,360]{1,0:T(8,128)}, f32[120,360]{1,0:T(8,128)}) custom-call(s32[9]{0:T(128)} %refs_0_.3, bf16[6,360,360]{2,1,0:T(8,128)(2,1)} %get-tuple-element.42.refs_1_, bf16[6,360,360]{2,1,0:T(8,128)(2,1)} %get-tuple-element.41.refs_2_, f32[120,384]{1,0:T(8,128)} %get-tuple-element.23.refs_3_, ...), custom_call_target="tpu_custom_call" | custom-call | tf_op jit(solution)/shard_map/pallas_call | solution.py:344
  40.4 0.5 collective-permute-done.11.refs_5_
  40.9 4.6 %shard_map.58 = (f32[60,360]{1,0:T(8,128)}, f32[60,360]{1,0:T(8,128)}, f32[60,360]{1,0:T(8,128)}, f32[60,360]{1,0:T(8,128)}) custom-call(s32[9]{0:T(128)} %refs_0_.3, bf16[6,360,360]{2,1,0:T(8,128)(2,1)} %get-tuple-element.42.refs_1_, bf16[6,360,360]{2,1,0:T(8,128)(2,1)} %get-tuple-element.41.refs_2_, f32[60,384]{1,0:T(8,128)} %get-tuple-element.31.refs_3_, ...), custom_call_target="tpu_custom_call" | custom-call | tf_op jit(solution)/shard_map/pallas_call | solution.py:344
  45.5 2.5 %collective-permute-start.13 = (f32[60,360]{1,0:T(8,128)}, f32[60,360]{1,0:T(8,128)S(1)}, u32[]{:S(2)}, u32[]{:S(2)}) collective-permute-start(f32[60,360]{1,0:T(8,128)} %get-tuple-element.36), channel_id=1, source_target_pairs={{0,1},{1,2},{2,3},{3,0},{4,5},{5,6},{6,7},{7,4},{8,9},{9,10},{10,1... | collective-permute-start | bytes 259208 | tf_op jit(solution)/shard_map/ppermute | solution.py:350
  48.0 0.2 collective-permute-start.7
  48.1 1.7 %collective-permute-start.8 = (f32[120,360]{1,0:T(8,128)S(1)}, f32[120,360]{1,0:T(8,128)S(1)}, u32[]{:S(2)}, u32[]{:S(2)}) collective-permute-start(f32[120,360]{1,0:T(8,128)S(1)} %copy-done.10), channel_id=1, source_target_pairs={{0,2},{1,3},{2,0},{3,1},{28,30},{29,31},{30,28},{31,29},{4,24},{5,... | collective-permute-start | bytes 518408 | tf_op jit(solution)/shard_map/ppermute | solution.py:350
  49.9 2.2 %collective-permute-start.9 = (f32[120,360]{1,0:T(8,128)S(1)}, f32[120,360]{1,0:T(8,128)S(1)}, u32[]{:S(2)}, u32[]{:S(2)}) collective-permute-start(f32[120,360]{1,0:T(8,128)S(1)} %copy-done.9), channel_id=1, source_target_pairs={{0,3},{1,0},{2,1},{3,2},{28,31},{29,28},{30,29},{31,30},{4,24},{5,... | collective-permute-start | bytes 518408 | tf_op jit(solution)/shard_map/ppermute | solution.py:350
  52.1 1.8 %collective-permute-start.14 = (f32[60,360]{1,0:T(8,128)}, f32[60,360]{1,0:T(8,128)S(1)}, u32[]{:S(2)}, u32[]{:S(2)}) collective-permute-start(f32[60,360]{1,0:T(8,128)} %get-tuple-element.37), channel_id=1, source_target_pairs={{0,2},{1,3},{2,0},{3,1},{4,6},{5,7},{6,4},{7,5},{8,10},{9,11},{10,... | collective-permute-start | bytes 259208 | tf_op jit(solution)/shard_map/ppermute | solution.py:350
  53.8 0.9 %collective-permute-start.15 = (f32[60,360]{1,0:T(8,128)}, f32[60,360]{1,0:T(8,128)S(1)}, u32[]{:S(2)}, u32[]{:S(2)}) collective-permute-start(f32[60,360]{1,0:T(8,128)} %get-tuple-element.38), channel_id=1, source_target_pairs={{0,3},{1,0},{2,1},{3,2},{4,7},{5,4},{6,5},{7,6},{8,11},{9,8},{10,9... | collective-permute-start | bytes 259208 | tf_op jit(solution)/shard_map/ppermute | solution.py:350
  54.7 11.1 %collective-permute-done.14.refs_7_ = f32[60,360]{1,0:T(8,128)S(1)} collective-permute-done((f32[60,360]{1,0:T(8,128)}, f32[60,360]{1,0:T(8,128)S(1)}, u32[]{:S(2)}, u32[]{:S(2)}) %collective-permute-start.14) | collective-permute-done | bytes 86432 | tf_op jit(solution)/shard_map/ppermute | solution.py:350
  65.9 0.6 copy-done.6
  66.7 2.8 %shard_map.59 = f32[9,80,360]{2,1,0:T(8,128)} custom-call(f32[9,80,360]{2,1,0:T(8,128)} %get-tuple-element.22.refs_0_, f32[120,360]{1,0:T(8,128)} %get-tuple-element.27.refs_1_, f32[120,360]{1,0:T(8,128)} %copy-done.1, f32[120,360]{1,0:T(8,128)} %copy-done.2, f32[120,360]{1,0:T(8,128)} %copy-done.3, f32[60,360]{1,0:T(8,128)} %get-tuple-element.35.refs_5_, ...), custom_call_target="tpu_custom_call" | custom-call | tf_op jit(solution)/shard_map/pallas_call | solution.py:355
  69.5 2.3 %copy.23 = f32[5,16,9,360]{3,1,2,0:T(8,128)} copy(f32[5,16,9,360]{3,1,0,2:T(8,128)} %bitcast.28) | data formatting | bytes 2073600 | tf_op jit(solution)/shard_map/reshape | solution.py:360
  (51 shorter events, 0.8 us)
Async XLA Ops:
  2.5 9.3 %copy-start = (f32[5,16,9,360]{3,1,0,2:T(8,128)}, f32[5,16,9,360]{3,1,0,2:T(8,128)S(1)}, u32[]{:S(2)}) copy-start(f32[5,16,9,360]{3,1,0,2:T(8,128)S(1)} %copy.18) | copy-start | bytes 3110404
  3.2 17.8 %collective-permute-start.3 = (f32[96,9]{1,0:T(8,128)S(1)}, f32[96,9]{1,0:T(8,128)}, u32[]{:S(2)}, u32[]{:S(2)}) collective-permute-start(f32[96,9]{1,0:T(8,128)S(1)} %copy.22), channel_id=1, source_target_pairs={{0,3},{1,0},{2,1},{3,2},{4,7},{5,4},{6,5},{7,6},{8,11},{9,8},{10,9... | collective-permute-start | bytes 10376 | tf_op jit(solution)/shard_map/ppermute | solution.py:327
  9.3 13.8 %collective-permute-start.2 = (f32[96,9]{1,0:T(8,128)}, f32[96,9]{1,0:T(8,128)}, u32[]{:S(2)}, u32[]{:S(2)}) collective-permute-start(f32[96,9]{1,0:T(8,128)} %copy.20), channel_id=1, source_target_pairs={{0,1},{1,2},{2,3},{3,0},{4,5},{5,6},{6,7},{7,4},{8,9},{9,10},{10,1... | collective-permute-start | bytes 10376 | tf_op jit(solution)/shard_map/ppermute | solution.py:326
  10.8 12.2 %collective-permute-start.1 = (f32[96,360]{1,0:T(8,128)}, f32[96,360]{1,0:T(8,128)}, u32[]{:S(2)}, u32[]{:S(2)}) collective-permute-start(f32[96,360]{1,0:T(8,128)} %get-tuple-element.45), channel_id=1, source_target_pairs={{0,4},{1,5},{2,6},{3,7},{4,0},{5,1},{6,2},{7,3},{8,12},{9,13},{10,... | collective-permute-start | bytes 414728 | tf_op jit(solution)/shard_map/ppermute | solution.py:312
  10.8 12.3 %collective-permute-start = (f32[96,360]{1,0:T(8,128)}, f32[96,360]{1,0:T(8,128)}, u32[]{:S(2)}, u32[]{:S(2)}) collective-permute-start(f32[96,360]{1,0:T(8,128)} %get-tuple-element.46), channel_id=1, source_target_pairs={{0,2},{1,3},{2,0},{3,1},{28,30},{29,31},{30,28},{31,29},{4,8},{8,4... | collective-permute-start | bytes 414728 | tf_op jit(solution)/shard_map/ppermute | solution.py:313
  15.4 16.2 %collective-permute-start.4 = (f32[120,384]{1,0:T(8,128)}, f32[120,384]{1,0:T(8,128)S(1)}, u32[]{:S(2)}, u32[]{:S(2)}) collective-permute-start(f32[120,384]{1,0:T(8,128)} %get-tuple-element.24), channel_id=1, source_target_pairs={{0,3},{1,0},{2,1},{3,2},{28,31},{29,28},{30,29},{31,30},{4,24},{5,... | collective-permute-start | bytes 552968 | tf_op jit(solution)/shard_map/ppermute | solution.py:321
  19.8 12.3 %copy-start.8 = (f32[6]{0:T(128)S(1)}, f32[6]{0:T(128)}, u32[]{:S(2)}) copy-start(f32[6]{0:T(128)} %constant.43.clone) | copy-start | bytes 76
  21.0 13.6 %collective-permute-start.5 = (f32[120,384]{1,0:T(8,128)}, f32[120,384]{1,0:T(8,128)}, u32[]{:S(2)}, u32[]{:S(2)}) collective-permute-start(f32[120,384]{1,0:T(8,128)} %get-tuple-element.25), channel_id=1, source_target_pairs={{0,2},{1,3},{2,0},{3,1},{28,30},{29,31},{30,28},{31,29},{4,24},{5,... | collective-permute-start | bytes 552968 | tf_op jit(solution)/shard_map/ppermute | solution.py:321
  23.1 11.5 %collective-permute-start.6 = (f32[120,384]{1,0:T(8,128)}, f32[120,384]{1,0:T(8,128)}, u32[]{:S(2)}, u32[]{:S(2)}) collective-permute-start(f32[120,384]{1,0:T(8,128)} %get-tuple-element.26), channel_id=1, source_target_pairs={{0,1},{1,2},{2,3},{3,0},{28,29},{29,30},{30,31},{31,28},{4,24},{5,... | collective-permute-start | bytes 552968 | tf_op jit(solution)/shard_map/ppermute | solution.py:321
  27.7 12.7 %collective-permute-start.10 = (f32[60,384]{1,0:T(8,128)}, f32[60,384]{1,0:T(8,128)}, u32[]{:S(2)}, u32[]{:S(2)}) collective-permute-start(f32[60,384]{1,0:T(8,128)} %get-tuple-element.32), channel_id=1, source_target_pairs={{0,3},{1,0},{2,1},{3,2},{4,7},{5,4},{6,5},{7,6},{8,11},{9,8},{10,9... | collective-permute-start | bytes 276488 | tf_op jit(solution)/shard_map/ppermute | solution.py:335
  31.5 9.4 %collective-permute-start.11 = (f32[60,384]{1,0:T(8,128)}, f32[60,384]{1,0:T(8,128)}, u32[]{:S(2)}, u32[]{:S(2)}) collective-permute-start(f32[60,384]{1,0:T(8,128)} %get-tuple-element.33), channel_id=1, source_target_pairs={{0,2},{1,3},{2,0},{3,1},{4,6},{5,7},{6,4},{7,5},{8,10},{9,11},{10,... | collective-permute-start | bytes 276488 | tf_op jit(solution)/shard_map/ppermute | solution.py:335
  31.5 3.0 %copy-start.4 = (f32[120,384]{1,0:T(8,128)}, f32[120,384]{1,0:T(8,128)S(1)}, u32[]{:S(2)}) copy-start(f32[120,384]{1,0:T(8,128)S(1)} %collective-permute-done.4.refs_4_) | copy-start | bytes 552964
  31.5 9.4 %collective-permute-start.12 = (f32[60,384]{1,0:T(8,128)}, f32[60,384]{1,0:T(8,128)}, u32[]{:S(2)}, u32[]{:S(2)}) collective-permute-start(f32[60,384]{1,0:T(8,128)} %get-tuple-element.34), channel_id=1, source_target_pairs={{0,1},{1,2},{2,3},{3,0},{4,5},{5,6},{6,7},{7,4},{8,9},{9,10},{10,1... | collective-permute-start | bytes 276488 | tf_op jit(solution)/shard_map/ppermute | solution.py:335
  40.4 7.6 %copy-start.11 = (f32[120,360]{1,0:T(8,128)S(1)}, f32[120,360]{1,0:T(8,128)}, u32[]{:S(2)}) copy-start(f32[120,360]{1,0:T(8,128)} %get-tuple-element.28) | copy-start | bytes 518404
  40.4 7.8 %copy-start.10 = (f32[120,360]{1,0:T(8,128)S(1)}, f32[120,360]{1,0:T(8,128)}, u32[]{:S(2)}) copy-start(f32[120,360]{1,0:T(8,128)} %get-tuple-element.29) | copy-start | bytes 518404
  40.4 9.5 %copy-start.9 = (f32[120,360]{1,0:T(8,128)S(1)}, f32[120,360]{1,0:T(8,128)}, u32[]{:S(2)}) copy-start(f32[120,360]{1,0:T(8,128)} %get-tuple-element.30) | copy-start | bytes 518404
  45.5 8.4 %collective-permute-start.13 = (f32[60,360]{1,0:T(8,128)}, f32[60,360]{1,0:T(8,128)S(1)}, u32[]{:S(2)}, u32[]{:S(2)}) collective-permute-start(f32[60,360]{1,0:T(8,128)} %get-tuple-element.36), channel_id=1, source_target_pairs={{0,1},{1,2},{2,3},{3,0},{4,5},{5,6},{6,7},{7,4},{8,9},{9,10},{10,1... | collective-permute-start | bytes 259208 | tf_op jit(solution)/shard_map/ppermute | solution.py:350
  48.0 17.8 %collective-permute-start.7 = (f32[120,360]{1,0:T(8,128)S(1)}, f32[120,360]{1,0:T(8,128)S(1)}, u32[]{:S(2)}, u32[]{:S(2)}) collective-permute-start(f32[120,360]{1,0:T(8,128)S(1)} %copy-done.11), channel_id=1, source_target_pairs={{0,1},{1,2},{2,3},{3,0},{28,29},{29,30},{30,31},{31,28},{4,24},{5,... | collective-permute-start | bytes 518408 | tf_op jit(solution)/shard_map/ppermute | solution.py:350
  48.1 17.7 %collective-permute-start.8 = (f32[120,360]{1,0:T(8,128)S(1)}, f32[120,360]{1,0:T(8,128)S(1)}, u32[]{:S(2)}, u32[]{:S(2)}) collective-permute-start(f32[120,360]{1,0:T(8,128)S(1)} %copy-done.10), channel_id=1, source_target_pairs={{0,2},{1,3},{2,0},{3,1},{28,30},{29,31},{30,28},{31,29},{4,24},{5,... | collective-permute-start | bytes 518408 | tf_op jit(solution)/shard_map/ppermute | solution.py:350
  49.9 16.0 %collective-permute-start.9 = (f32[120,360]{1,0:T(8,128)S(1)}, f32[120,360]{1,0:T(8,128)S(1)}, u32[]{:S(2)}, u32[]{:S(2)}) collective-permute-start(f32[120,360]{1,0:T(8,128)S(1)} %copy-done.9), channel_id=1, source_target_pairs={{0,3},{1,0},{2,1},{3,2},{28,31},{29,28},{30,29},{31,30},{4,24},{5,... | collective-permute-start | bytes 518408 | tf_op jit(solution)/shard_map/ppermute | solution.py:350
  52.1 13.8 %collective-permute-start.14 = (f32[60,360]{1,0:T(8,128)}, f32[60,360]{1,0:T(8,128)S(1)}, u32[]{:S(2)}, u32[]{:S(2)}) collective-permute-start(f32[60,360]{1,0:T(8,128)} %get-tuple-element.37), channel_id=1, source_target_pairs={{0,2},{1,3},{2,0},{3,1},{4,6},{5,7},{6,4},{7,5},{8,10},{9,11},{10,... | collective-permute-start | bytes 259208 | tf_op jit(solution)/shard_map/ppermute | solution.py:350
  53.8 12.0 %copy-start.5 = (f32[60,360]{1,0:T(8,128)}, f32[60,360]{1,0:T(8,128)S(1)}, u32[]{:S(2)}) copy-start(f32[60,360]{1,0:T(8,128)S(1)} %collective-permute-done.13.refs_6_) | copy-start | bytes 259204
  53.8 12.0 %collective-permute-start.15 = (f32[60,360]{1,0:T(8,128)}, f32[60,360]{1,0:T(8,128)S(1)}, u32[]{:S(2)}, u32[]{:S(2)}) collective-permute-start(f32[60,360]{1,0:T(8,128)} %get-tuple-element.38), channel_id=1, source_target_pairs={{0,3},{1,0},{2,1},{3,2},{4,7},{5,4},{6,5},{7,6},{8,11},{9,8},{10,9... | collective-permute-start | bytes 259208 | tf_op jit(solution)/shard_map/ppermute | solution.py:350
  65.8 0.6 copy-start.6
  65.8 0.7 copy-start.7
  65.8 0.7 %copy-start.1 = (f32[120,360]{1,0:T(8,128)}, f32[120,360]{1,0:T(8,128)S(1)}, u32[]{:S(2)}) copy-start(f32[120,360]{1,0:T(8,128)S(1)} %collective-permute-done.7.refs_2_) | copy-start | bytes 518404
  65.9 0.8 %copy-start.2 = (f32[120,360]{1,0:T(8,128)}, f32[120,360]{1,0:T(8,128)S(1)}, u32[]{:S(2)}) copy-start(f32[120,360]{1,0:T(8,128)S(1)} %collective-permute-done.8.refs_3_) | copy-start | bytes 518404
  65.9 0.8 %copy-start.3 = (f32[120,360]{1,0:T(8,128)}, f32[120,360]{1,0:T(8,128)S(1)}, u32[]{:S(2)}) copy-start(f32[120,360]{1,0:T(8,128)S(1)} %collective-permute-done.9.refs_4_) | copy-start | bytes 518404

commit v3 on v0

v3 whole, which is shorter than its diff:
```python
import math

import jax
import jax.numpy as jnp
from jax import lax
from jax.experimental import pallas as pl
from jax.experimental.pallas import tpu as pltpu
from jax.sharding import PartitionSpec as P

LANES = 128
EDGES = 4
FINE = 16


def padded(n):
    return -(-n // LANES) * LANES


class Plan:
    def __init__(self, fields, levels, rows, sector, n_lat, n_lon):
        self.fields, self.levels, self.rows, self.sector = fields, levels, rows, sector
        self.n_lat, self.n_lon = n_lat, n_lon
        self.planes = fields * levels
        self.circle = sector * n_lon
        self.quarter = self.circle // 4
        self.size = padded(self.quarter)
        cap = rows * n_lat // 6
        self.full = (cap - 1) // rows
        self.n_x = cap - self.full * rows
        self.n_y = rows - self.n_x
        self.width = padded(sector + EDGES)
        self.x_count = self.n_x * self.planes // n_lon
        self.y_count = self.n_y * self.planes // n_lon
        self.x_full = [0] + list(range(1 + self.n_y, rows))

    def pieces(self, index, count):
        start, out = index * self.planes, []
        stop = start + self.planes
        while start < stop:
            chunk, offset = divmod(start, count)
            size = min(count - offset, stop - start)
            out.append((chunk, offset, start - index * self.planes, size))
            start += size
        return out

    def is_full(self, lat):
        return (lat < self.full) | (lat >= self.n_lat - self.full)

    def is_part(self, lat):
        return (lat == self.full) | (lat == self.n_lat - 1 - self.full)

    def x_row(self, index, lat):
        south = lat >= self.n_lat // 2
        partial = jnp.where(south, self.rows - self.n_x + index, index)
        return jnp.where(self.is_full(lat), self.x_full[index], partial)

    def y_row(self, index, lat):
        return 1 + index


def split_speed(speed):
    return jnp.maximum(speed, 0.0), jnp.minimum(speed, 0.0)


def tiled(x, fields):
    return jnp.concatenate([x] * fields, axis=0) if fields > 1 else x


def back(x):
    return pltpu.roll(x, x.shape[1] - 1, 1)


def row_of(plan, q_ref, r):
    return q_ref[:, pl.ds(r, 1)].reshape(plan.planes, plan.sector)


def face_flux(plan, v_low, v_high, q_low, q_high):
    plus, minus = split_speed(0.5 * (v_low + v_high))
    return tiled(plus, plan.fields) * q_low + tiled(minus, plan.fields) * q_high


def first_kernel(plan, q_ref, u_ref, v_ref, *refs):
    n = plan.n_lon
    outs, (one, two, first, last, buf, q_pad, u_pad) = refs[:n], refs[n:]
    width, sector, planes = plan.width, plan.sector, plan.planes
    odd = lax.rem(lax.axis_index("lat"), 2) == 1
    lon = lax.axis_index("lon")
    lane = lax.broadcasted_iota(jnp.int32, (plan.levels, width), 1)
    inside = lane < sector - 1
    base = sector // LANES * LANES
    tail_lane = base + lax.broadcasted_iota(jnp.int32, (planes, width - base), 1)
    q_pad[...] = jnp.zeros_like(q_pad)
    u_pad[...] = jnp.zeros_like(u_pad)
    q_rows = [row_of(plan, q_ref, r) for r in range(plan.rows)]

    def south_flux(r):
        return face_flux(plan, v_ref[r], v_ref[r + 1], q_rows[r], q_rows[r + 1])

    north = south_flux(0)
    for i in range(plan.n_y):
        r = 1 + i
        q_pad[:, 0:sector] = q_rows[r]
        u_pad[:, 0:sector] = u_ref[r]
        q, u = q_pad[...], u_pad[...]
        plus, minus = split_speed(0.5 * (u + back(u)))
        plus, minus = jnp.where(inside, plus, 0.0), jnp.where(inside, minus, 0.0)
        east = tiled(plus, plan.fields) * q + tiled(minus, plan.fields) * back(q)
        stepped = q - (east - pltpu.roll(east, 1, 1))
        south = south_flux(r)
        q_pad[...] = stepped
        q_pad[:, 0:sector] = q_pad[:, 0:sector] - (south - north)
        tail = q_pad[:, base:]
        for k, value in enumerate(
            (q[:, 0:1], q[:, sector - 1 : sector], tiled(u[:, 0:1], plan.fields), tiled(u[:, sector - 1 : sector], plan.fields))
        ):
            tail = jnp.where(tail_lane == sector + k, value, tail)
        q_pad[:, base:] = tail
        for chunk, offset, start, size in plan.pieces(i, plan.y_count):
            buf[chunk, offset : offset + size, :] = q_pad[start : start + size, :]
        north = south
    for s in range(n):
        outs[s][...] = buf[lax.rem(lon + s, n)]

    one[0:planes, :] = jnp.where(odd, q_rows[-1], q_rows[0])
    one[planes:, :] = jnp.where(odd, v_ref[plan.rows - 1], v_ref[0])
    two[0:planes, :] = jnp.where(odd, q_rows[0], q_rows[-1])
    two[planes:, :] = jnp.where(odd, v_ref[0], v_ref[plan.rows - 1])
    for r in range(plan.rows):
        for out, at in ((first, 0), (last, sector - 1)):
            out[0:planes, r : r + 1] = q_rows[r][:, at : at + 1]
            out[planes:, r : r + 1] = u_ref[r][:, at : at + 1]


def ghosts(plan, one_ref, two_ref):
    lat = lax.axis_index("lat")
    odd = lax.rem(lat, 2) == 1
    sign_north = jnp.where(lat == 0, -1.0, 1.0)
    sign_south = jnp.where(lat == plan.n_lat - 1, -1.0, 1.0)
    one, two, planes = one_ref[...], two_ref[...], plan.planes
    above, below = jnp.where(odd, two, one), jnp.where(odd, one, two)
    return above[:planes], above[planes:] * sign_north, below[:planes], below[planes:] * sign_south


def lon_step(plan, q_pad, u_pad, q_row, u_row, east_column, west_column):
    sector, width, planes = plan.sector, plan.width, plan.planes
    q_pad[:, 0:sector] = q_row
    u_pad[:, 0:sector] = u_row
    q_pad[:, sector : sector + 1] = east_column[:planes]
    u_pad[:, sector : sector + 1] = east_column[planes:]
    q_pad[:, width - 1 : width] = west_column[:planes]
    u_pad[:, width - 1 : width] = west_column[planes:]
    q, u = q_pad[...], u_pad[...]
    plus, minus = split_speed(0.5 * (u + back(u)))
    east = tiled(plus, plan.fields) * q + tiled(minus, plan.fields) * back(q)
    return q - (east - pltpu.roll(east, 1, 1))


def travelling_kernel(plan, q_ref, u_ref, v_ref, one_ref, two_ref, west_ref, east_ref, *refs):
    n = plan.n_lon
    outs, (buf, q_pad, u_pad) = refs[:n], refs[n:]
    sector, rows = plan.sector, plan.rows
    lat, lon = lax.axis_index("lat"), lax.axis_index("lon")
    q_above, v_above, q_below, v_below = ghosts(plan, one_ref, two_ref)
    q_pad[...] = jnp.zeros_like(q_pad)
    u_pad[...] = jnp.zeros_like(u_pad)
    lane = lax.broadcasted_iota(jnp.int32, east_ref.shape, 1)

    def column(ref, r):
        return jnp.sum(jnp.where(lane == r, ref[...], 0.0), axis=1, keepdims=True)

    for j in range(plan.n_x):
        r = plan.x_row(j, lat)
        before, after = jnp.maximum(r - 1, 0), jnp.minimum(r + 1, rows - 1)
        top, bottom = r == 0, r == rows - 1
        q_row, v_row = row_of(plan, q_ref, r), v_ref[r]
        stepped = lon_step(plan, q_pad, u_pad, q_row, u_ref[r], column(east_ref, r), column(west_ref, r))
        south = face_flux(
            plan,
            v_row,
            jnp.where(bottom, v_below, v_ref[after]),
            q_row,
            jnp.where(bottom, q_below, row_of(plan, q_ref, after)),
        )
        north = face_flux(
            plan,
            jnp.where(top, v_above, v_ref[before]),
            v_row,
            jnp.where(top, q_above, row_of(plan, q_ref, before)),
            q_row,
        )
        q_pad[...] = stepped
        q_pad[:, 0:sector] = q_pad[:, 0:sector] - (south - north)
        for chunk, offset, start, size in plan.pieces(j, plan.x_count):
            buf[chunk, offset : offset + size, :] = q_pad[start : start + size, :]
    for s in range(n):
        outs[s][...] = buf[lax.rem(lon + s, n)]


def rest_kernel(plan, q_ref, u_ref, v_ref, one_ref, two_ref, west_ref, east_ref, out, q_pad, u_pad):
    sector, rows = plan.sector, plan.rows

    @pl.when(jnp.logical_not(plan.is_full(lax.axis_index("lat"))))
    def _():
        q_above, v_above, q_below, v_below = ghosts(plan, one_ref, two_ref)
        q_pad[...] = jnp.zeros_like(q_pad)
        u_pad[...] = jnp.zeros_like(u_pad)
        north = face_flux(plan, v_above, v_ref[0], q_above, row_of(plan, q_ref, 0))
        for r in range(rows):
            q_row = row_of(plan, q_ref, r)
            stepped = lon_step(
                plan, q_pad, u_pad, q_row, u_ref[r], east_ref[:, r : r + 1], west_ref[:, r : r + 1]
            )
            inner = r + 1 < rows
            south = face_flux(
                plan,
                v_ref[r],
                v_ref[r + 1] if inner else v_below,
                q_row,
                row_of(plan, q_ref, r + 1) if inner else q_below,
            )
            value = stepped[:, 0:sector] - (south - north)
            out[:, r : r + 1] = value.reshape(plan.fields, 1, plan.levels, sector)
            north = south


def turn(numerator, circle):
    p = numerator - circle * jnp.floor(numerator * (1.0 / circle))
    j = jnp.floor(p * (4.0 / circle) + 0.5)
    x = (p - j * (circle / 4)) * (2.0 * math.pi / circle)
    z = x * x
    s = x * (1 + z * (-1 / 6 + z * (1 / 120 + z * (-1 / 5040 + z * (1 / 362880)))))
    c = 1 + z * (-1 / 2 + z * (1 / 24 + z * (-1 / 720 + z * (1 / 40320 + z * (-1 / 3628800)))))
    swap = (j == 1.0) | (j == 3.0)
    cos, sin = jnp.where(swap, s, c), jnp.where(swap, c, s)
    cos = jnp.where((j == 1.0) | (j == 2.0), -cos, cos)
    sin = jnp.where((j == 2.0) | (j == 3.0), -sin, sin)
    return cos, sin


def table_kernel(plan, even_hi, even_lo, odd_hi, odd_lo):
    size = plan.size
    coarse = size // FINE

    def numerators(count, step, r):
        n = step * lax.broadcasted_iota(jnp.int32, (count, size), 0)
        k = 4 * lax.broadcasted_iota(jnp.int32, (count, size), 1) + r
        return (n * k).astype(jnp.float32)

    def put(hi, lo, index, value):
        high = value.astype(jnp.bfloat16)
        hi[index] = high
        lo[index] = (value - high.astype(jnp.float32)).astype(jnp.bfloat16)

    for r in range(4):
        cos_c, sin_c = turn(numerators(coarse, FINE, r), plan.circle)
        cos_f, sin_f = turn(numerators(FINE, 1, r), plan.circle)
        sum_f, gap_f = cos_f + sin_f, cos_f - sin_f
        column = slice(0, size) if r < 2 else slice(size, 2 * size)
        for i in range(coarse):
            c, s = cos_c[i : i + 1], sin_c[i : i + 1]
            rows = slice(i * FINE, (i + 1) * FINE)
            plus = c * sum_f + s * gap_f
            if r % 2 == 0:
                put(even_hi, even_lo, (r // 2, rows), plus)
            else:
                minus = c * gap_f - s * sum_f
                put(odd_hi, odd_lo, (rows, column), plus)
                rows = slice(size + i * FINE, size + (i + 1) * FINE)
                put(odd_hi, odd_lo, (rows, column), minus if r == 1 else -minus)


def product(x, table_hi, table_lo, transposed):
    dims = (((1,), (1 if transposed else 0,)), ((), ()))
    x_hi = x.astype(jnp.bfloat16)
    x_lo = (x - x_hi.astype(jnp.float32)).astype(jnp.bfloat16)
    count = x.shape[0]
    both = lax.dot_general(
        jnp.concatenate([x_hi, x_lo], axis=0), table_hi, dims, preferred_element_type=jnp.float32
    )
    low = lax.dot_general(x_hi, table_lo, dims, preferred_element_type=jnp.float32)
    return both[:count] + both[count:] + low


def filter_quarters(plan, quarters, cut, even_hi, even_lo, odd_hi, odd_lo):
    x0, x1, x2, x3 = quarters
    size, circle = plan.size, plan.circle
    a, b, odd = x0 + x2, x1 + x3, jnp.concatenate([x0 - x2, x1 - x3], axis=1)

    def kept(h, k, m):
        ok = (jnp.minimum(k, circle - k) <= cut) & (m < plan.quarter)
        return jnp.where(ok, h, 0.0) * (1.0 / circle)

    m = lax.broadcasted_iota(jnp.int32, x0.shape, 1)
    lane = lax.broadcasted_iota(jnp.int32, odd.shape, 1)
    m_odd = jnp.where(lane < size, lane, lane - size)
    k_odd = 4 * m_odd + jnp.where(lane < size, 1, 3)
    tables = [(even_hi[0], even_lo[0]), (even_hi[1], even_lo[1]), (odd_hi[...], odd_lo[...])]
    h0 = kept(product(a + b, *tables[0], False), 4 * m, m)
    h2 = kept(product(a - b, *tables[1], False), 4 * m + 2, m)
    h13 = kept(product(odd, *tables[2], False), k_odd, m_odd)
    even, twice = product(h0, *tables[0], True), product(h2, *tables[1], True)
    other = product(h13, *tables[2], True)
    both, apart = even + twice, even - twice
    o_u, o_v = other[:, :size], other[:, size:]
    return both + o_u, apart + o_v, both - o_u, apart - o_v


def filter_kernel(plan, count, rows_here, row_index, with_edges, needed, cut_ref, *refs):
    n = plan.n_lon
    tables, ins, outs = refs[:4], refs[4 : 4 + n], refs[4 + n :]
    sector, width = plan.sector, plan.width
    lat, lon = lax.axis_index("lat"), lax.axis_index("lon")

    @pl.when(needed(lat))
    def _():
        circle_index = lon * count + lax.broadcasted_iota(jnp.int32, (count, 1), 0)
        cut = jnp.full((count, 1), plan.circle, jnp.int32)
        for i in range(rows_here):
            here = (circle_index >= i * plan.planes) & (circle_index < (i + 1) * plan.planes)
            cut = jnp.where(here, cut_ref[row_index(i, lat)], cut)
        lane = lax.broadcasted_iota(jnp.int32, (count, width), 1)
        pieces = [jnp.where(lane < sector, ref[...], 0.0) for ref in ins]
        if with_edges:
            tails = [ref[:, sector : sector + EDGES] for ref in ins]
            fluxes = []
            for j in range(n):
                here, there = tails[j], tails[(j + 1) % n]
                plus, minus = split_speed(0.5 * (here[:, 3:4] + there[:, 2:3]))
                fluxes.append(plus * here[:, 1:2] + minus * there[:, 0:1])
            pieces = [
                piece
                - jnp.where(lane == sector - 1, fluxes[j], 0.0)
                + jnp.where(lane == 0, fluxes[j - 1], 0.0)
                for j, piece in enumerate(pieces)
            ]
        per = n // 4
        if per == 1 and width == plan.size:
            quarters = pieces
        else:
            spare = [jnp.zeros((count, plan.size - plan.quarter), jnp.float32)] * (plan.size > plan.quarter)
            quarters = [
                jnp.concatenate([p[:, :sector] for p in pieces[per * i : per * (i + 1)]] + spare, axis=1)
                for i in range(4)
            ]
        filtered = filter_quarters(plan, quarters, cut, *tables)
        for j in range(n):
            part = j % per
            outs[j][:, 0:sector] = filtered[j // per][:, part * sector : (part + 1) * sector]


def place_kernel(plan, count, rows_here, row_index, needed, whole, *refs):
    n = plan.n_lon
    ins, (out, buf, row_buf, sems) = refs[:n], refs[n:]
    lat, lon = lax.axis_index("lat"), lax.axis_index("lon")

    @pl.when(needed(lat))
    def _():
        for j in range(n):
            buf[lax.rem(lon + n - j, n)] = ins[j][...]
        copies = []
        for i in range(rows_here):
            for chunk, offset, start, size in plan.pieces(i, count):
                row_buf[i, start : start + size, :] = buf[chunk, offset : offset + size, 0 : plan.sector]
            for f in range(plan.fields):
                copies.append(
                    pltpu.make_async_copy(
                        row_buf.at[i, pl.ds(f * plan.levels, plan.levels)],
                        out.at[f, row_index(i, lat)],
                        sems.at[i, f],
                    )
                )
                copies[-1].start()
        for copy in copies:
            copy.wait()


def f32(*shape):
    return jax.ShapeDtypeStruct(shape, jnp.float32)


def vmem(*shape):
    return pltpu.VMEM(shape, jnp.float32)


def body(tracers, zonal_wind, meridional_wind, cutoff):
    fields, levels, rows, sector = tracers.shape
    n_lat, n_lon = lax.axis_size("lat"), lax.axis_size("lon")
    plan = Plan(fields, levels, rows, sector, n_lat, n_lon)
    planes, width, size = plan.planes, plan.width, plan.size
    q = jnp.transpose(tracers, (0, 2, 1, 3))
    u, v = (jnp.transpose(x, (1, 0, 2)) for x in (zonal_wind, meridional_wind))
    both = ("lat", "lon")

    def device(lat, lon):
        return lat * n_lon + lon % n_lon

    def shift_pairs(lats, by):
        return [(device(a, z), device(a, z + by)) for a in lats for z in range(n_lon)]

    def x_pairs(by):
        return shift_pairs(range(n_lat), by)

    def swapped(a, b):
        return [(device(p, z), device(q, z)) for p, q in ((a, b), (b, a)) for z in range(n_lon)]

    def y_pairs(by):
        spare = list(range(plan.full + 1, n_lat - plan.full - 1))
        pairs = shift_pairs(list(range(plan.full)) + list(range(n_lat - plan.full, n_lat)), by)
        pairs += swapped(plan.full, n_lat - 1 - plan.full)
        for a, b in zip(spare[0::2], spare[1::2]):
            pairs += swapped(a, b)
        return pairs

    pairs_one = shift_pairs((0, n_lat - 1), n_lon // 2)
    for a in range(1, n_lat - 1, 2):
        pairs_one += swapped(a, a + 1)
    pairs_two = [pair for a in range(0, n_lat, 2) for pair in swapped(a, a + 1)]

    *y_send, to_one, to_two, first, last = pl.pallas_call(
        lambda *refs: first_kernel(plan, *refs),
        out_shape=[f32(plan.y_count, width)] * n_lon
        + [f32(planes + levels, sector)] * 2
        + [f32(planes + levels, rows)] * 2,
        scratch_shapes=[vmem(n_lon, plan.y_count, width), vmem(planes, width), vmem(levels, width)],
        name="inner",
    )(q, u, v)
    y_got = [y_send[0]] + [lax.ppermute(y_send[s], both, y_pairs(s)) for s in range(1, n_lon)]
    two = lax.ppermute(to_two, both, pairs_two)
    one = lax.ppermute(to_one, both, pairs_one)
    west = lax.ppermute(last, both, x_pairs(1))
    east = lax.ppermute(first, both, x_pairs(-1))

    *x_send, = pl.pallas_call(
        lambda *refs: travelling_kernel(plan, *refs),
        out_shape=[f32(plan.x_count, width)] * n_lon,
        scratch_shapes=[vmem(n_lon, plan.x_count, width), vmem(planes, width), vmem(levels, width)],
        name="travel",
    )(q, u, v, one, two, west, east)
    x_got = [x_send[0]] + [lax.ppermute(x_send[s], both, x_pairs(s)) for s in range(1, n_lon)]

    out = pl.pallas_call(
        lambda *refs: rest_kernel(plan, *refs),
        out_shape=f32(fields, rows, levels, sector),
        scratch_shapes=[vmem(planes, width), vmem(levels, width)],
        name="rest",
    )(q, u, v, one, two, west, east)

    tables = pl.pallas_call(
        lambda *refs: table_kernel(plan, *refs),
        out_shape=[jax.ShapeDtypeStruct((2, size, size), jnp.bfloat16)] * 2
        + [jax.ShapeDtypeStruct((2 * size, 2 * size), jnp.bfloat16)] * 2,
        name="tables",
    )()
    whole = pl.BlockSpec(memory_space=pltpu.VMEM)
    smem = pl.BlockSpec(memory_space=pltpu.SMEM)
    anywhere = pl.BlockSpec(memory_space=pl.ANY)

    def filtered(got, count, rows_here, row_index, with_edges, needed, pairs, name):
        ordered = [got[(n_lon - j) % n_lon] for j in range(n_lon)]
        pieces = pl.pallas_call(
            lambda *refs: filter_kernel(plan, count, rows_here, row_index, with_edges, needed, *refs),
            out_shape=[f32(count, width)] * n_lon,
            in_specs=[smem] + [whole] * (4 + n_lon),
            name=name,
        )(cutoff, *tables, *ordered)
        return [pieces[0]] + [lax.ppermute(pieces[s], both, pairs(s)) for s in range(1, n_lon)]

    def placed(out, pieces, count, rows_here, row_index, needed, name):
        return pl.pallas_call(
            lambda *refs: place_kernel(plan, count, rows_here, row_index, needed, *refs),
            out_shape=f32(fields, rows, levels, sector),
            in_specs=[anywhere] + [whole] * n_lon,
            out_specs=anywhere,
            scratch_shapes=[
                vmem(n_lon, count, width),
                vmem(rows_here, planes, sector),
                pltpu.SemaphoreType.DMA((rows_here, fields)),
            ],
            input_output_aliases={0: 0},
            name=name,
        )(out, *pieces)

    def polar(lat):
        return plan.is_full(lat) | plan.is_part(lat)

    y_args = plan.y_count, plan.n_y, plan.y_row
    x_args = plan.x_count, plan.n_x, plan.x_row
    y_back = filtered(y_got, *y_args, True, plan.is_full, y_pairs, "filter_y")
    x_back = filtered(x_got, *x_args, False, polar, x_pairs, "filter_x")
    out = placed(out, y_back, *y_args, plan.is_full, "place_y")
    out = placed(out, x_back, *x_args, polar, "place_x")
    return jnp.transpose(out, (0, 2, 1, 3))


def solution(mesh):
    in_specs = (P(None, None, "lat", "lon"), P(None, "lat", "lon"), P(None, "lat", "lon"), P("lat"))
    out_specs = P(None, None, "lat", "lon")
    return jax.shard_map(body, mesh=mesh, in_specs=in_specs, out_specs=out_specs, check_vma=False)
```

time: 138 us -> 69.2 us (0.50)
  blocking collectives: 29.4 us -> 0 us
  other arithmetic: 26.6 us -> 0 us
  Pallas kernels: 0 us -> 26.4 us
  waiting for transfers between devices: 31.1 us -> 12.1 us
  matrix products: 15.3 us -> 0 us
  local copies, waits for them, and re-layouts: 15.7 us -> 4.14 us
  starting transfers between devices: 18.4 us -> 26.1 us
    all_to_all x1 -> x0, blocking collectives: 29.4 us -> none  [body(): lax.all_to_all(done, 'lon', split_axis=1, concat_axis=0, tiled=True)]
    pallas_call x0 -> x8, Pallas kernels: none -> 26.4 us  [the longest x2 10.2 us: filtered(): pl.pallas_call(lambda *refs: filter_kernel(plan, count, rows_here, row_in...]
    all_to_all x1 -> x0, waiting for transfers between devices: 26.1 us -> none  [body(): share = lax.all_to_all(flat, 'lon', split_axis=0, concat_axis=1, tiled=True)]
    sin x1 -> x0, other arithmetic: 18.4 us -> none  [table_rows(): return jnp.concatenate([jnp.cos(phase), jnp.sin(phase)], axis=1)]
    ppermute x5 -> x16, starting transfers between devices: 10.1 us -> 26.1 us  [the longest x6 9.36 us: filtered(): lax.ppermute(pieces[s], both, pairs(s))]
    dot_general x2 -> x0, matrix products: 15.3 us -> none  [the longest x1 8.49 us: inverse_rows(): lax.dot_general(scaled, table, (((1,), (1,)), ((), ())), precision=lax.Pr...]
    all_to_all x1 -> x0, starting transfers between devices: 8.33 us -> none  [body(): share = lax.all_to_all(flat, 'lon', split_axis=0, concat_axis=1, tiled=True)]
    ppermute x5 -> x16, waiting for transfers between devices: 4.98 us -> 12.1 us  [the longest x3 5.01 us: body(): lax.ppermute(x_send[s], both, x_pairs(s))]
  transfers between devices with their start and end apart: 6 -> 16, of which waited for: 3 -> 3; matrix products, arithmetic and copies ran while one was open for 5% -> 0% of each run, Pallas kernels for 0% -> 30%
where the time goes in v3:
time: 69.2 us; the launch traced here: 69 us
  Pallas kernels  26.4 us (38%)
  starting transfers between devices  26.1 us (38%)
  waiting for transfers between devices  12.1 us (17%)
  local copies, waits for them, and re-layouts  4.14 us (6%)
    pallas_call x2, Pallas kernels, filtered(): pl.pallas_call(lambda *refs: filter_kernel(plan, count, rows_here, row_in...  10.2 us
    ppermute x6, starting transfers between devices, filtered(): lax.ppermute(pieces[s], both, pairs(s))  9.36 us
    ppermute x3, starting transfers between devices, body(): lax.ppermute(y_send[s], both, y_pairs(s))  6.09 us
    ppermute x3, waiting for transfers between devices, body(): lax.ppermute(x_send[s], both, x_pairs(s))  5.01 us
    ppermute x1, waiting for transfers between devices, body(): west = lax.ppermute(last, both, x_pairs(1))  4.91 us
    ppermute x1, starting transfers between devices, body(): one = lax.ppermute(to_one, both, pairs_one)  4.49 us
    pallas_call x2, Pallas kernels, placed(): pl.pallas_call(lambda *refs: place_kernel(plan, count, rows_here, row_ind...  4.27 us
    unnamed x36, local copies, waits for them, and re-layouts  4.14 us
  transfers between devices with their start and end apart: 16, of which 3 were waited for; matrix products, arithmetic and copies ran while one was open for 0% of the time, Pallas kernels for 30%

profile of v3, /device:TPU:0, one launch (start us, length us, event | category | flops | bytes accessed | tf_op | source)
XLA Modules:
  0.0 69.0 jit_solution(3497958146277652639)
XLA Ops:
  0.0 3.6 %inner.1 = (f32[120,384]{1,0:T(8,128)}, f32[120,384]{1,0:T(8,128)}, f32[120,384]{1,0:T(8,128)}, f32[120,384]{1,0:T(8,128)}, f32[96,360]{1,0:T(8,128)}, /*index=5...) custom-call(f32[5,9,16,360]{3,2,1,0:T(8,128)} %bitcast.4, f32[9,16,360]{2,1,0:T(8,128)} %bitcast.7, f32[9,16,360]{2,1,0:T(8,128)} %bitcast.10), custom_call_target="tpu_custom_call" | custom-call | tf_op jit(solution)/shard_map/inner/pallas_call | solution.py:419
  3.6 5.1 %collective-permute-start.4 = (f32[120,384]{1,0:T(8,128)}, f32[120,384]{1,0:T(8,128)S(1)}, u32[]{:S(2)}, u32[]{:S(2)}) collective-permute-start(f32[120,384]{1,0:T(8,128)} %get-tuple-element.38), channel_id=1, source_target_pairs={{0,3},{1,0},{2,1},{3,2},{28,31},{29,28},{30,29},{31,30},{4,24},{5,... | collective-permute-start | bytes 552968 | tf_op jit(solution)/shard_map/ppermute | solution.py:427
  8.7 1.0 %collective-permute-start.6 = (f32[120,384]{1,0:T(8,128)}, f32[120,384]{1,0:T(8,128)S(1)}, u32[]{:S(2)}, u32[]{:S(2)}) collective-permute-start(f32[120,384]{1,0:T(8,128)} %get-tuple-element.40), channel_id=1, source_target_pairs={{0,1},{1,2},{2,3},{3,0},{28,29},{29,30},{30,31},{31,28},{4,24},{5,... | collective-permute-start | bytes 552968 | tf_op jit(solution)/shard_map/ppermute | solution.py:427
  9.7 2.5 %collective-permute-start.2 = (f32[96,9]{1,0:T(8,128)}, f32[96,9]{1,0:T(8,128)S(1)}, u32[]{:S(2)}, u32[]{:S(2)}) collective-permute-start(f32[96,9]{1,0:T(8,128)} %get-tuple-element.31), channel_id=1, source_target_pairs={{0,1},{1,2},{2,3},{3,0},{4,5},{5,6},{6,7},{7,4},{8,9},{9,10},{10,1... | collective-permute-start | bytes 10376 | tf_op jit(solution)/shard_map/ppermute | solution.py:430
  12.1 1.3 %collective-permute-start.3 = (f32[96,9]{1,0:T(8,128)}, f32[96,9]{1,0:T(8,128)S(1)}, u32[]{:S(2)}, u32[]{:S(2)}) collective-permute-start(f32[96,9]{1,0:T(8,128)} %get-tuple-element.32), channel_id=1, source_target_pairs={{0,3},{1,0},{2,1},{3,2},{4,7},{5,4},{6,5},{7,6},{8,11},{9,8},{10,9... | collective-permute-start | bytes 10376 | tf_op jit(solution)/shard_map/ppermute | solution.py:431
  13.5 4.9 %collective-permute-done.2.refs_5_ = f32[96,9]{1,0:T(8,128)S(1)} collective-permute-done((f32[96,9]{1,0:T(8,128)}, f32[96,9]{1,0:T(8,128)S(1)}, u32[]{:S(2)}, u32[]{:S(2)}) %collective-permute-start.2) | collective-permute-done | bytes 3488 | tf_op jit(solution)/shard_map/ppermute | solution.py:430
  18.4 4.5 %collective-permute-start = (f32[96,360]{1,0:T(8,128)}, f32[96,360]{1,0:T(8,128)S(1)}, u32[]{:S(2)}, u32[]{:S(2)}) collective-permute-start(f32[96,360]{1,0:T(8,128)} %get-tuple-element.29), channel_id=1, source_target_pairs={{0,2},{1,3},{2,0},{3,1},{28,30},{29,31},{30,28},{31,29},{4,8},{5,9... | collective-permute-start | bytes 414728 | tf_op jit(solution)/shard_map/ppermute | solution.py:429
  22.9 2.7 %tables.1 = (bf16[2,384,384]{2,1,0:T(8,128)(2,1)}, bf16[2,384,384]{2,1,0:T(8,128)(2,1)}, bf16[768,768]{1,0:T(8,128)(2,1)}, bf16[768,768]{1,0:T(8,128)(2,1)}) custom-call(), custom_call_target="tpu_custom_call" | custom-call | tf_op jit(solution)/shard_map/tables/pallas_call | solution.py:448
  25.6 2.2 %collective-permute-done.refs_3_ = f32[96,360]{1,0:T(8,128)S(1)} collective-permute-done((f32[96,360]{1,0:T(8,128)}, f32[96,360]{1,0:T(8,128)S(1)}, u32[]{:S(2)}, u32[]{:S(2)}) %collective-permute-start) | collective-permute-done | bytes 138272 | tf_op jit(solution)/shard_map/ppermute | solution.py:429
  27.8 0.6 copy-done
  28.5 0.7 copy-done.1
  29.1 3.1 %travel.1 = (f32[60,384]{1,0:T(8,128)}, f32[60,384]{1,0:T(8,128)}, f32[60,384]{1,0:T(8,128)}, f32[60,384]{1,0:T(8,128)}) custom-call(f32[5,9,16,360]{3,2,1,0:T(8,128)} %bitcast.5, f32[9,16,360]{2,1,0:T(8,128)} %bitcast.8, f32[9,16,360]{2,1,0:T(8,128)} %bitcast.11, f32[96,360]{1,0:T(8,128)} %copy-done, f32[96,360]{1,0:T(8,128)} %copy-done.1, ...), custom_call_target="tpu_custom_call" | custom-call | tf_op jit(solution)/shard_map/travel/pallas_call | solution.py:433
  32.2 0.6 copy-done.7
  32.9 0.1 copy-done.8
  32.9 0.1 copy-done.9
  33.0 5.6 %filter_y.1 = (f32[120,384]{1,0:T(8,128)}, f32[120,384]{1,0:T(8,128)}, f32[120,384]{1,0:T(8,128)}, f32[120,384]{1,0:T(8,128)}) custom-call(s32[9]{0:T(128)} %refs_0_.3, bf16[2,384,384]{2,1,0:T(8,128)(2,1)} %get-tuple-element.33.refs_1_, bf16[2,384,384]{2,1,0:T(8,128)(2,1)} %get-tuple-element.34.refs_2_, bf16[768,768]{1,0:T(8,128)(2,1)} %get-tuple-element.35.refs_3_, ...), custom_call_target="tpu_custom_call" | custom-call | tf_op jit(solution)/shard_map/filter_y/pallas_call | solution.py:460
  38.6 2.0 %collective-permute-start.7 = (f32[120,384]{1,0:T(8,128)}, f32[120,384]{1,0:T(8,128)S(1)}, u32[]{:S(2)}, u32[]{:S(2)}) collective-permute-start(f32[120,384]{1,0:T(8,128)} %get-tuple-element.42), channel_id=1, source_target_pairs={{0,1},{1,2},{2,3},{3,0},{28,29},{29,30},{30,31},{31,28},{4,24},{5,... | collective-permute-start | bytes 552968 | tf_op jit(solution)/shard_map/ppermute | solution.py:466
  40.6 1.3 %collective-permute-start.11 = (f32[60,384]{1,0:T(8,128)S(1)}, f32[60,384]{1,0:T(8,128)S(1)}, u32[]{:S(2)}, u32[]{:S(2)}) collective-permute-start(f32[60,384]{1,0:T(8,128)S(1)} %copy-done.17), channel_id=1, source_target_pairs={{0,2},{1,3},{2,0},{3,1},{4,6},{5,7},{6,4},{7,5},{8,10},{9,11},{10,... | collective-permute-start | bytes 276488 | tf_op jit(solution)/shard_map/ppermute | solution.py:439
  42.0 1.0 %collective-permute-start.12 = (f32[60,384]{1,0:T(8,128)S(1)}, f32[60,384]{1,0:T(8,128)S(1)}, u32[]{:S(2)}, u32[]{:S(2)}) collective-permute-start(f32[60,384]{1,0:T(8,128)S(1)} %copy-done.16), channel_id=1, source_target_pairs={{0,1},{1,2},{2,3},{3,0},{4,5},{5,6},{6,7},{7,4},{8,9},{9,10},{10,1... | collective-permute-start | bytes 276488 | tf_op jit(solution)/shard_map/ppermute | solution.py:439
  43.0 0.6 collective-permute-start.8
  43.6 2.9 %collective-permute-start.9 = (f32[120,384]{1,0:T(8,128)}, f32[120,384]{1,0:T(8,128)S(1)}, u32[]{:S(2)}, u32[]{:S(2)}) collective-permute-start(f32[120,384]{1,0:T(8,128)} %get-tuple-element.44), channel_id=1, source_target_pairs={{0,3},{1,0},{2,1},{3,2},{28,31},{29,28},{30,29},{31,30},{4,24},{5,... | collective-permute-start | bytes 552968 | tf_op jit(solution)/shard_map/ppermute | solution.py:466
  46.5 5.0 %collective-permute-done.11.refs_7_ = f32[60,384]{1,0:T(8,128)S(1)} collective-permute-done((f32[60,384]{1,0:T(8,128)S(1)}, f32[60,384]{1,0:T(8,128)S(1)}, u32[]{:S(2)}, u32[]{:S(2)}) %collective-permute-start.11) | collective-permute-done | bytes 92192 | tf_op jit(solution)/shard_map/ppermute | solution.py:439
  51.5 0.6 copy-done.14
  52.2 4.7 %filter_x.1 = (f32[60,384]{1,0:T(8,128)}, f32[60,384]{1,0:T(8,128)}, f32[60,384]{1,0:T(8,128)}, f32[60,384]{1,0:T(8,128)}) custom-call(s32[9]{0:T(128)} %refs_0_.3, bf16[2,384,384]{2,1,0:T(8,128)(2,1)} %get-tuple-element.33.refs_1_, bf16[2,384,384]{2,1,0:T(8,128)(2,1)} %get-tuple-element.34.refs_2_, bf16[768,768]{1,0:T(8,128)(2,1)} %get-tuple-element.35.refs_3_, ...), custom_call_target="tpu_custom_call" | custom-call | tf_op jit(solution)/shard_map/filter_x/pallas_call | solution.py:460
  56.8 0.1 collective-permute-start.14
  56.9 3.8 %collective-permute-start.15 = (f32[60,384]{1,0:T(8,128)}, f32[60,384]{1,0:T(8,128)S(1)}, u32[]{:S(2)}, u32[]{:S(2)}) collective-permute-start(f32[60,384]{1,0:T(8,128)} %get-tuple-element.52), channel_id=1, source_target_pairs={{0,3},{1,0},{2,1},{3,2},{4,7},{5,4},{6,5},{7,6},{8,11},{9,8},{10,9... | collective-permute-start | bytes 276488 | tf_op jit(solution)/shard_map/ppermute | solution.py:466
  60.7 2.5 %rest.1.refs_0_ = f32[5,9,16,360]{3,2,1,0:T(8,128)} custom-call(f32[5,9,16,360]{3,2,1,0:T(8,128)} %bitcast.6, f32[9,16,360]{2,1,0:T(8,128)} %bitcast.9, f32[9,16,360]{2,1,0:T(8,128)} %bitcast.12, f32[96,360]{1,0:T(8,128)} %copy-done, f32[96,360]{1,0:T(8,128)} %copy-done.1, f32[96,9]{1,0:T(8,128)} %copy-done.2, f32[96,9]{1,0:T(8,128)} %copy-done.3), custom_call_target="tpu_custom_call" | custom-call | tf_op jit(solution)/shard_map/rest/pallas_call | solution.py:441
  63.2 0.6 copy-done.5
  63.9 0.1 copy-done.6
  64.0 2.3 %place_y.1.refs_0_ = f32[5,9,16,360]{3,2,1,0:T(8,128)} custom-call(f32[5,9,16,360]{3,2,1,0:T(8,128)} %rest.1.refs_0_, f32[120,384]{1,0:T(8,128)} %get-tuple-element.41.refs_1_, f32[120,384]{1,0:T(8,128)} %copy-done.4, f32[120,384]{1,0:T(8,128)} %copy-done.5, f32[120,384]{1,0:T(8,128)} %copy-done.6), custom_call_target="tpu_custom_call", output_to_operand_aliasing={{}: (0, {})} | custom-call | tf_op jit(solution)/shard_map/place_y/pallas_call | solution.py:469
  66.4 0.6 copy-done.10
  67.0 1.9 %place_x.1 = f32[5,9,16,360]{3,2,1,0:T(8,128)} custom-call(f32[5,9,16,360]{3,2,1,0:T(8,128)} %place_y.1.refs_0_, f32[60,384]{1,0:T(8,128)} %get-tuple-element.49.refs_1_, f32[60,384]{1,0:T(8,128)} %copy-done.10, f32[60,384]{1,0:T(8,128)} %copy-done.11, f32[60,384]{1,0:T(8,128)} %copy-done.12), custom_call_target="tpu_custom_call", output_to_operand_aliasing={{}: (0, {})} | custom-call | tf_op jit(solution)/shard_map/place_x/pallas_call | solution.py:469
  (44 shorter events, 0.2 us)
Async XLA Ops:
  3.6 28.6 %collective-permute-start.4 = (f32[120,384]{1,0:T(8,128)}, f32[120,384]{1,0:T(8,128)S(1)}, u32[]{:S(2)}, u32[]{:S(2)}) collective-permute-start(f32[120,384]{1,0:T(8,128)} %get-tuple-element.38), channel_id=1, source_target_pairs={{0,3},{1,0},{2,1},{3,2},{28,31},{29,28},{30,29},{31,30},{4,24},{5,... | collective-permute-start | bytes 552968 | tf_op jit(solution)/shard_map/ppermute | solution.py:427
  8.7 23.5 %collective-permute-start.5 = (f32[120,384]{1,0:T(8,128)}, f32[120,384]{1,0:T(8,128)S(1)}, u32[]{:S(2)}, u32[]{:S(2)}) collective-permute-start(f32[120,384]{1,0:T(8,128)} %get-tuple-element.39), channel_id=1, source_target_pairs={{0,2},{1,3},{2,0},{3,1},{28,30},{29,31},{30,28},{31,29},{4,24},{5,... | collective-permute-start | bytes 552968 | tf_op jit(solution)/shard_map/ppermute | solution.py:427
  8.7 23.6 %collective-permute-start.6 = (f32[120,384]{1,0:T(8,128)}, f32[120,384]{1,0:T(8,128)S(1)}, u32[]{:S(2)}, u32[]{:S(2)}) collective-permute-start(f32[120,384]{1,0:T(8,128)} %get-tuple-element.40), channel_id=1, source_target_pairs={{0,1},{1,2},{2,3},{3,0},{28,29},{29,30},{30,31},{31,28},{4,24},{5,... | collective-permute-start | bytes 552968 | tf_op jit(solution)/shard_map/ppermute | solution.py:427
  9.7 8.7 %collective-permute-start.2 = (f32[96,9]{1,0:T(8,128)}, f32[96,9]{1,0:T(8,128)S(1)}, u32[]{:S(2)}, u32[]{:S(2)}) collective-permute-start(f32[96,9]{1,0:T(8,128)} %get-tuple-element.31), channel_id=1, source_target_pairs={{0,1},{1,2},{2,3},{3,0},{4,5},{5,6},{6,7},{7,4},{8,9},{9,10},{10,1... | collective-permute-start | bytes 10376 | tf_op jit(solution)/shard_map/ppermute | solution.py:430
  12.1 10.7 %collective-permute-start.3 = (f32[96,9]{1,0:T(8,128)}, f32[96,9]{1,0:T(8,128)S(1)}, u32[]{:S(2)}, u32[]{:S(2)}) collective-permute-start(f32[96,9]{1,0:T(8,128)} %get-tuple-element.32), channel_id=1, source_target_pairs={{0,3},{1,0},{2,1},{3,2},{4,7},{5,4},{6,5},{7,6},{8,11},{9,8},{10,9... | collective-permute-start | bytes 10376 | tf_op jit(solution)/shard_map/ppermute | solution.py:431
  18.4 9.4 %copy-start.2 = (f32[96,9]{1,0:T(8,128)}, f32[96,9]{1,0:T(8,128)S(1)}, u32[]{:S(2)}) copy-start(f32[96,9]{1,0:T(8,128)S(1)} %collective-permute-done.2.refs_5_) | copy-start | bytes 10372
  18.4 9.4 %collective-permute-start = (f32[96,360]{1,0:T(8,128)}, f32[96,360]{1,0:T(8,128)S(1)}, u32[]{:S(2)}, u32[]{:S(2)}) collective-permute-start(f32[96,360]{1,0:T(8,128)} %get-tuple-element.29), channel_id=1, source_target_pairs={{0,2},{1,3},{2,0},{3,1},{28,30},{29,31},{30,28},{31,29},{4,8},{5,9... | collective-permute-start | bytes 414728 | tf_op jit(solution)/shard_map/ppermute | solution.py:429
  22.9 4.9 %copy-start.3 = (f32[96,9]{1,0:T(8,128)}, f32[96,9]{1,0:T(8,128)S(1)}, u32[]{:S(2)}) copy-start(f32[96,9]{1,0:T(8,128)S(1)} %collective-permute-done.3.refs_6_) | copy-start | bytes 10372
  22.9 4.9 %collective-permute-start.1 = (f32[96,360]{1,0:T(8,128)}, f32[96,360]{1,0:T(8,128)S(1)}, u32[]{:S(2)}, u32[]{:S(2)}) collective-permute-start(f32[96,360]{1,0:T(8,128)} %get-tuple-element.30), channel_id=1, source_target_pairs={{0,4},{1,5},{2,6},{3,7},{4,0},{5,1},{6,2},{7,3},{8,12},{9,13},{10,... | collective-permute-start | bytes 414728 | tf_op jit(solution)/shard_map/ppermute | solution.py:428
  27.8 0.7 copy-start
  28.5 0.7 copy-start.1
  32.2 11.4 %collective-permute-start.10 = (f32[60,384]{1,0:T(8,128)}, f32[60,384]{1,0:T(8,128)S(1)}, u32[]{:S(2)}, u32[]{:S(2)}) collective-permute-start(f32[60,384]{1,0:T(8,128)} %get-tuple-element.46), channel_id=1, source_target_pairs={{0,3},{1,0},{2,1},{3,2},{4,7},{5,4},{6,5},{7,6},{8,11},{9,8},{10,9... | collective-permute-start | bytes 276488 | tf_op jit(solution)/shard_map/ppermute | solution.py:439
  32.2 0.7 copy-start.7
  32.2 0.7 %copy-start.8 = (f32[120,384]{1,0:T(8,128)}, f32[120,384]{1,0:T(8,128)S(1)}, u32[]{:S(2)}) copy-start(f32[120,384]{1,0:T(8,128)S(1)} %collective-permute-done.5.refs_7_) | copy-start | bytes 552964
  32.2 0.8 %copy-start.9 = (f32[120,384]{1,0:T(8,128)}, f32[120,384]{1,0:T(8,128)S(1)}, u32[]{:S(2)}) copy-start(f32[120,384]{1,0:T(8,128)S(1)} %collective-permute-done.6.refs_8_) | copy-start | bytes 552964
  33.0 7.6 %copy-start.17 = (f32[60,384]{1,0:T(8,128)S(1)}, f32[60,384]{1,0:T(8,128)}, u32[]{:S(2)}) copy-start(f32[60,384]{1,0:T(8,128)} %get-tuple-element.47) | copy-start | bytes 276484
  33.0 8.9 %copy-start.16 = (f32[60,384]{1,0:T(8,128)S(1)}, f32[60,384]{1,0:T(8,128)}, u32[]{:S(2)}) copy-start(f32[60,384]{1,0:T(8,128)} %get-tuple-element.48) | copy-start | bytes 276484
  38.6 18.3 %collective-permute-start.7 = (f32[120,384]{1,0:T(8,128)}, f32[120,384]{1,0:T(8,128)S(1)}, u32[]{:S(2)}, u32[]{:S(2)}) collective-permute-start(f32[120,384]{1,0:T(8,128)} %get-tuple-element.42), channel_id=1, source_target_pairs={{0,1},{1,2},{2,3},{3,0},{28,29},{29,30},{30,31},{31,28},{4,24},{5,... | collective-permute-start | bytes 552968 | tf_op jit(solution)/shard_map/ppermute | solution.py:466
  40.6 10.9 %collective-permute-start.11 = (f32[60,384]{1,0:T(8,128)S(1)}, f32[60,384]{1,0:T(8,128)S(1)}, u32[]{:S(2)}, u32[]{:S(2)}) collective-permute-start(f32[60,384]{1,0:T(8,128)S(1)} %copy-done.17), channel_id=1, source_target_pairs={{0,2},{1,3},{2,0},{3,1},{4,6},{5,7},{6,4},{7,5},{8,10},{9,11},{10,... | collective-permute-start | bytes 276488 | tf_op jit(solution)/shard_map/ppermute | solution.py:439
  42.0 9.5 %collective-permute-start.12 = (f32[60,384]{1,0:T(8,128)S(1)}, f32[60,384]{1,0:T(8,128)S(1)}, u32[]{:S(2)}, u32[]{:S(2)}) collective-permute-start(f32[60,384]{1,0:T(8,128)S(1)} %copy-done.16), channel_id=1, source_target_pairs={{0,1},{1,2},{2,3},{3,0},{4,5},{5,6},{6,7},{7,4},{8,9},{9,10},{10,1... | collective-permute-start | bytes 276488 | tf_op jit(solution)/shard_map/ppermute | solution.py:439
  43.0 20.2 %collective-permute-start.8 = (f32[120,384]{1,0:T(8,128)}, f32[120,384]{1,0:T(8,128)S(1)}, u32[]{:S(2)}, u32[]{:S(2)}) collective-permute-start(f32[120,384]{1,0:T(8,128)} %get-tuple-element.43), channel_id=1, source_target_pairs={{0,2},{1,3},{2,0},{3,1},{28,30},{29,31},{30,28},{31,29},{4,24},{5,... | collective-permute-start | bytes 552968 | tf_op jit(solution)/shard_map/ppermute | solution.py:466
  43.6 7.9 %copy-start.13 = (f32[60,384]{1,0:T(8,128)}, f32[60,384]{1,0:T(8,128)S(1)}, u32[]{:S(2)}) copy-start(f32[60,384]{1,0:T(8,128)S(1)} %collective-permute-done.10.refs_6_) | copy-start | bytes 276484
  43.6 19.6 %collective-permute-start.9 = (f32[120,384]{1,0:T(8,128)}, f32[120,384]{1,0:T(8,128)S(1)}, u32[]{:S(2)}, u32[]{:S(2)}) collective-permute-start(f32[120,384]{1,0:T(8,128)} %get-tuple-element.44), channel_id=1, source_target_pairs={{0,3},{1,0},{2,1},{3,2},{28,31},{29,28},{30,29},{31,30},{4,24},{5,... | collective-permute-start | bytes 552968 | tf_op jit(solution)/shard_map/ppermute | solution.py:466
  51.5 0.7 copy-start.15
  56.8 9.5 %collective-permute-start.13 = (f32[60,384]{1,0:T(8,128)}, f32[60,384]{1,0:T(8,128)S(1)}, u32[]{:S(2)}, u32[]{:S(2)}) collective-permute-start(f32[60,384]{1,0:T(8,128)} %get-tuple-element.50), channel_id=1, source_target_pairs={{0,1},{1,2},{2,3},{3,0},{4,5},{5,6},{6,7},{7,4},{8,9},{9,10},{10,1... | collective-permute-start | bytes 276488 | tf_op jit(solution)/shard_map/ppermute | solution.py:466
  56.8 9.5 %collective-permute-start.14 = (f32[60,384]{1,0:T(8,128)}, f32[60,384]{1,0:T(8,128)S(1)}, u32[]{:S(2)}, u32[]{:S(2)}) collective-permute-start(f32[60,384]{1,0:T(8,128)} %get-tuple-element.51), channel_id=1, source_target_pairs={{0,2},{1,3},{2,0},{3,1},{4,6},{5,7},{6,4},{7,5},{8,10},{9,11},{10,... | collective-permute-start | bytes 276488 | tf_op jit(solution)/shard_map/ppermute | solution.py:466
  56.9 6.3 %copy-start.4 = (f32[120,384]{1,0:T(8,128)}, f32[120,384]{1,0:T(8,128)S(1)}, u32[]{:S(2)}) copy-start(f32[120,384]{1,0:T(8,128)S(1)} %collective-permute-done.7.refs_2_) | copy-start | bytes 552964
  56.9 9.4 %collective-permute-start.15 = (f32[60,384]{1,0:T(8,128)}, f32[60,384]{1,0:T(8,128)S(1)}, u32[]{:S(2)}, u32[]{:S(2)}) collective-permute-start(f32[60,384]{1,0:T(8,128)} %get-tuple-element.52), channel_id=1, source_target_pairs={{0,3},{1,0},{2,1},{3,2},{4,7},{5,4},{6,5},{7,6},{8,11},{9,8},{10,9... | collective-permute-start | bytes 276488 | tf_op jit(solution)/shard_map/ppermute | solution.py:466
  63.2 0.7 copy-start.5
  63.2 0.7 %copy-start.6 = (f32[120,384]{1,0:T(8,128)}, f32[120,384]{1,0:T(8,128)S(1)}, u32[]{:S(2)}) copy-start(f32[120,384]{1,0:T(8,128)S(1)} %collective-permute-done.9.refs_4_) | copy-start | bytes 552964
  66.3 0.6 copy-start.11
  66.4 0.7 copy-start.12
  (2 other events, 1.3 us)
